TPU v7x, 512 devices: a whole 4x8x8 slice. The times are simulated.
512 devices in a mesh: ply: 8 (over y_lo, x), stripe: 64 (over z, y_hi, core).
Axes of the slice: x: 4, y: 8 (y_hi: 4, y_lo: 2; y = y_hi * 2 + y_lo), z: 8, core: 2. Of those that a mesh axis runs over, the one named last changes fastest.
Arguments:
- displacement: float32 [3, 8, 4, 512, 512], P(None, 'ply', None, 'stripe'), may hold values from -5 to 5
- velocity: float32 [3, 8, 4, 512, 512], P(None, 'ply', None, 'stripe'), may hold values from -5 to 5
- acceleration: float32 [3, 8, 4, 512, 512], P(None, 'ply', None, 'stripe'), may hold values from -5 to 5
- fibre_codes: int32 [8, 2], P('ply'), may hold values from 0 to 3
- contact_mask: int32 [512, 512], P('stripe'), may hold values 0 or 1
- bond_flags: int32 [8, 2, 64, 64], P('ply', None, 'stripe'), may hold values from 0 to 1073741823, as said below
Outputs:
- new_displacement: float32 [3, 8, 4, 512, 512], P(None, 'ply', None, 'stripe')
- new_velocity: float32 [3, 8, 4, 512, 512], P(None, 'ply', None, 'stripe')
- new_acceleration: float32 [3, 8, 4, 512, 512], P(None, 'ply', None, 'stripe')
Inputs may be any that keep to these rules, and one draw needn't show every extreme that they name: `fibre_codes`: codes 0, 1, 2 and 3 stand for fibres at 0, 90, 45 and -45 degrees in the pair's frame. `contact_mask`: a point in contact with the impactor is 1. `bond_flags`: word 0 holds classes 0 to 29 in bits 0 to 29, word 1 classes 30 to 46 in bits 0 to 16; higher bits are zero; in every draw one block of the lowest pair has all its bonds to the pair above broken.
All inputs are finite; a program needn't handle non-finite values. No bound on the sum of `contact_mask` on one device may be relied on, other than what follows from the above.
Results may differ from a plain program's by a relative error of at most 0.0003.
Values sent between devices are 32-bit elements; how exact they have to be, the bound alone decides.
No kernel may reach another device: no remote copies, remote signals or barrier semaphores. Data moves between devices by JAX's collectives and lax.ppermute only.
A program may use at most 64 MiB of HBM per device.

v0:
```python
import jax
import jax.numpy as jnp
from jax import lax
from jax.experimental import pallas as pl
from jax.experimental.pallas import tpu as pltpu
from jax.sharding import PartitionSpec as P

ROOT_HALF = 0.7071067811865476
RATE = 0.025
MATRIX_C = 1.0
FIBRE_C = 4.0
INTER_C = 1.5
IMPACT = 2.0

F32 = jnp.float32
I32 = jnp.int32
ROWS = 8
TURNS = 64
CELLS = ROWS * TURNS
WINDOW = 12
PLANE = [(di, dj) for di in range(-2, 3) for dj in range(-2, 3)]
INTERPRET = False


def place():
    return lax.axis_index("ply"), lax.axis_index("stripe")


def class_index(dz, di, dj):
    count = 0
    for z in range(1, 4):
        for i in range(-3, 4):
            for j in range(-3, 4):
                if z * z + i * i + j * j <= 9:
                    if (z, i, j) == (dz, di, dj):
                        return count
                    count += 1
    raise ValueError("no class")


def kernel_call(body, outs, scratch, flops):
    return pl.pallas_call(
        body,
        out_shape=outs,
        scratch_shapes=scratch,
        interpret=INTERPRET,
        cost_estimate=pl.CostEstimate(flops=flops, bytes_accessed=2_000_000, transcendentals=0),
        compiler_params=pltpu.CompilerParams(vmem_limit_bytes=32 * 1024 * 1024),
    )


def scaled(factor, value):
    if factor == 1:
        return value
    if factor == -1:
        return -value
    return factor * value


def along(di, dj, first, second):
    if di == 0 and dj == 0:
        return None
    if di == 0:
        return scaled(dj, second)
    if dj == 0:
        return scaled(di, first)
    if abs(di) == abs(dj):
        inner = first + second if di == dj else first - second
        return scaled(di, inner)
    return scaled(di, first) + scaled(dj, second)


def gap(far, near, rise, far_z, near_z):
    total = None if far is None else far - near
    if rise:
        lift = scaled(rise, far_z - near_z)
        total = lift if total is None else total + lift
    return total


def added(total, value):
    return value if total is None else total + value


def lanes_and_cells():
    cell = lax.broadcasted_iota(I32, (8, 128), 0)
    lane = lax.broadcasted_iota(I32, (8, 128), 1)
    return cell, lane


def shifted_by(value, cell):
    after = pltpu.roll(value, 127, 1)
    before = pltpu.roll(value, 1, 1)
    moved = {}
    for dj in (1, 2):
        moved[dj] = pltpu.roll(jnp.where(cell < dj, after, value), 8 - dj, 0)
        moved[-dj] = pltpu.roll(jnp.where(cell >= 8 - dj, before, value), dj, 0)
    return moved, after, before


def advance_kernel(disp, vel, acc, flags, adv, half, down, up, low, high):
    values = []
    for layer in range(4):
        for comp in range(3):
            speed = vel[comp, 0, layer] + 0.5 * acc[comp, 0, layer]
            moved = disp[comp, 0, layer] + speed
            half[comp, 0, layer] = speed
            adv[comp, 0, layer] = moved
            field = 3 * layer + comp
            low[field] = moved[5:8]
            high[field] = moved[0:3]
            values.append(moved)
    for slot, field in enumerate((1, 0, 2, 4, 3, 5, 8)):
        down[8 * slot : 8 * slot + 8] = values[field]
    for slot, field in enumerate((10, 9, 11, 7, 6, 8, 5)):
        up[8 * slot : 8 * slot + 8] = values[field]
    first = flags[0, 0]
    second = flags[0, 1]
    parts = jnp.concatenate(
        [jnp.bitwise_and(first, 0x7FFF), jnp.right_shift(first, 15), second, jnp.zeros((5, TURNS), I32)],
        axis=0,
    ).astype(F32)
    block = lax.broadcasted_iota(I32, (TURNS, CELLS), 0)
    column = lax.broadcasted_iota(I32, (TURNS, CELLS), 1)
    spread = (jnp.right_shift(column, 3) == block).astype(F32)
    up[56:64] = jnp.dot(parts, spread, precision=lax.Precision.HIGHEST, preferred_element_type=F32)


def turn_kernel(above, below, message, turned):
    stacked = jnp.concatenate([above[...], below[...], jnp.zeros((8, CELLS), F32)], axis=0)
    turned[0:8] = jnp.zeros((8, 128), F32)
    turned[CELLS + 8 : CELLS + 16] = jnp.zeros((8, 128), F32)
    for piece in range(4):
        turned[8 + 128 * piece : 136 + 128 * piece] = stacked[:, 128 * piece : 128 * piece + 128].T
    for row in range(WINDOW):
        message[pl.ds(row, TURNS, stride=WINDOW), :] = turned[pl.ds(6 + row, TURNS, stride=8), :]


def coefficient(here, there, dz, di, dj):
    radius = float(dz * dz + di * di + dj * dj)
    level = RATE / radius**1.5
    return level * MATRIX_C + (level * FIBRE_C * 0.5 / radius) * (here + there)


def pair_kernel(adv, low, high, codes, flags, force, own, words, natural, turned, held, moved, far, rates, present, spare):
    ply, stripe = place()
    cell, lane = lanes_and_cells()
    for field in range(12):
        comp, layer = field % 3, field // 3
        whole = adv[comp, 0, layer]
        natural[0, 10 * field : 10 * field + 3] = low[field]
        natural[0, 10 * field + 3 : 10 * field + 10] = whole[0:7]
        natural[1, 10 * field : 10 * field + 7] = whole[1:8]
        natural[1, 10 * field + 7 : 10 * field + 10] = high[field]
    for side in range(2):
        natural[side, 120:128] = jnp.zeros((8, CELLS), F32)
        for piece in range(4):
            turned[side, 128 * piece : 128 * piece + 128] = natural[side, :, 128 * piece : 128 * piece + 128].T
    for position in range(8):
        pick = pl.ds(position, TURNS, stride=8)
        both = jnp.concatenate([turned[0, pick, :], turned[1, pick, :]], axis=0)
        held[128 * position : 128 * position + 128] = both.T
    for field in range(12):
        for q in range(-3, 7):
            value = held[pl.ds(10 * field + q + 3, 8, stride=128), :]
            moved[2, field, q + 3] = value
            if 0 <= q < 4:
                own[field, q] = value
            if -2 <= q < 6:
                others, after, before = shifted_by(value, cell)
                for dj, other in others.items():
                    moved[dj + 2, field, q + 3] = other
                if field % 3 == 1 and 0 <= q < 4:
                    far[0, field // 3, q] = pltpu.roll(jnp.where(cell >= 5, before, value), 3, 0)
                    far[1, field // 3, q] = pltpu.roll(jnp.where(cell < 3, after, value), 5, 0)
    row = 8 * stripe + jnp.where(lane >= TURNS, 4, 0)
    column = 8 * jnp.bitwise_and(lane, TURNS - 1) + cell
    row_in = [(row + q >= 0) & (row + q < CELLS) for q in range(-3, 7)]
    for dj in range(-3, 4):
        column_in = (column + dj >= 0) & (column + dj < CELLS)
        for q in range(-3, 7):
            present[dj + 3, q + 3] = (row_in[q + 3] & column_in).astype(F32)
    spare[0:1, 0:TURNS] = flags[0, 0]
    spare[1:2, 0:TURNS] = flags[0, 1]
    both = spare[...]
    both = jnp.where(lane < TURNS, both, pltpu.roll(both, TURNS, 1))
    no_upper = ply == lax.axis_size("ply") - 1 if not INTERPRET else ply == 7
    for word in range(2):
        plain = jnp.broadcast_to(both[word : word + 1], (8, 128))
        for dj in range(-2, 3):
            column_in = (column + dj >= 0) & (column + dj < CELLS)
            for q in range(8):
                good = row_in[q + 1] & column_in & jnp.logical_not(no_upper)
                words[word, dj + 2, q] = jnp.where(good, plain, -1)
    cos_parts, sin_parts = [], []
    for side in range(2):
        code = codes[0, side]
        cosine = jnp.where(code == 0, 1.0, jnp.where(code == 1, 0.0, ROOT_HALF))
        sine = jnp.where(code == 0, 0.0, jnp.where(code == 1, 1.0, jnp.where(code == 2, ROOT_HALF, -ROOT_HALF)))
        cos_parts.append(jnp.full((8, 128), cosine, F32))
        sin_parts.append(jnp.full((8, 128), sine, F32))
    for place_index, (di, dj) in enumerate(PLANE):
        lean = [(di * cos_parts[side] + dj * sin_parts[side]) ** 2 for side in range(2)]
        if (di, dj) != (0, 0):
            rates[place_index, 0] = coefficient(lean[0], lean[0], 0, di, dj)
            rates[place_index, 1] = coefficient(lean[1], lean[1], 0, di, dj)
        rates[place_index, 2] = coefficient(lean[0], lean[0], 1, di, dj)
        rates[place_index, 3] = coefficient(lean[0], lean[1], 1, di, dj)
        rates[place_index, 4] = coefficient(lean[1], lean[1], 1, di, dj)
        rates[place_index, 5] = coefficient(lean[0], lean[1], 2, di, dj)
    for side in range(2):
        lean = (3 * cos_parts[side]) ** 2
        rates[25, side] = 9.0 * coefficient(lean, lean, 0, 3, 0)
        lean = (3 * sin_parts[side]) ** 2
        rates[25, 2 + side] = 9.0 * coefficient(lean, lean, 0, 0, 3)
    rates[25, 4] = 9.0 * coefficient(jnp.zeros((8, 128), F32), 0.0, 3, 0, 0)

    def bonds(m, carry):
        x = [moved[2, field, m + 3] for field in range(12)]
        total = [None] * 12
        for place_index, (di, dj) in enumerate(PLANE):
            y = [moved[dj + 2, field, m + 3 + di] for field in range(12)]
            far_e = [along(di, dj, y[3 * l], y[3 * l + 1]) for l in range(4)]
            near_e = [along(di, dj, x[3 * l], x[3 * l + 1]) for l in range(4)]
            here = present[dj + 3, m + 3 + di]
            for layer in range(4):
                plane, lift, double = None, None, None
                for other in range(4):
                    dz = other - layer
                    if dz * dz + di * di + dj * dj > 9 or (dz, di, dj) == (0, 0, 0) or abs(dz) == 3:
                        continue
                    pick = {0: layer // 2, 1: 2 + (layer + other) // 2, 2: 5}[abs(dz)]
                    if abs(dz) == 1:
                        pick = 2 + min(layer, other)
                    s = gap(far_e[other], near_e[layer], dz, y[3 * other + 2], x[3 * layer + 2])
                    t = rates[place_index, pick] * s
                    plane = added(plane, t)
                    if abs(dz) == 1:
                        lift = added(lift, t if dz > 0 else -t)
                    if abs(dz) == 2:
                        lift = added(lift, scaled(dz, t))
                if di or dj:
                    plane = plane * here
                    if di:
                        total[3 * layer] = added(total[3 * layer], scaled(di, plane))
                    if dj:
                        total[3 * layer + 1] = added(total[3 * layer + 1], scaled(dj, plane))
                total[3 * layer + 2] = added(total[3 * layer + 2], lift * here)
        rise = rates[25, 4] * (x[11] - x[2])
        total[2] = total[2] + rise
        total[11] = total[11] - rise
        for layer in range(4):
            for side, step in ((0, -3), (1, 3)):
                apart = present[3, m + 3 + step] * (moved[2, 3 * layer, m + 3 + step] - x[3 * layer])
                total[3 * layer] = total[3 * layer] + rates[25, layer // 2] * apart
                apart = present[3 + step, m + 3] * (far[side, layer, m] - x[3 * layer + 1])
                total[3 * layer + 1] = total[3 * layer + 1] + rates[25, 2 + layer // 2] * apart
        for field in range(12):
            force[field, m] = total[field]
        return carry

    lax.fori_loop(0, 4, bonds, 0)


def interface_kernel(message, own, words, force, half, mask, new_v, new_a, facing, moved, below, shared, turned):
    ply, stripe = place()
    cell, lane = lanes_and_cells()
    for q in range(8):
        both = jnp.concatenate(
            [message[pl.ds(q, TURNS, stride=WINDOW), :], message[pl.ds(q + 4, TURNS, stride=WINDOW), :]], axis=0
        )
        facing[q] = both.T
    for q in range(8):
        for slot in range(13):
            if slot == 6:
                continue
            field = facing[q, 8 * slot : 8 * slot + 8]
            moved[2, slot, q] = field
            for dj, other in shifted_by(field, cell)[0].items():
                moved[dj + 2, slot, q] = other
    row = 8 * stripe + jnp.where(lane >= TURNS, 4, 0)
    column = 8 * jnp.bitwise_and(lane, TURNS - 1) + cell
    for source, spots in ((0, (0, 1)), (2, (2, 3, 4, 5)), (6, (6, 7))):
        parts = facing[source, 112:120].astype(I32)
        joined = [jnp.bitwise_or(jnp.left_shift(parts[1:2], 15), parts[0:1]), parts[2:3]]
        for word in range(2):
            plain = jnp.broadcast_to(joined[word], (8, 128))
            before, after = pltpu.roll(plain, 1, 1), pltpu.roll(plain, 127, 1)
            for dj in range(-2, 3):
                turned_word = plain
                if dj < 0:
                    turned_word = jnp.where(cell + dj < 0, before, plain)
                if dj > 0:
                    turned_word = jnp.where(cell + dj > 7, after, plain)
                column_in = (column + dj >= 0) & (column + dj < CELLS) & (ply > 0)
                for q in spots:
                    good = (row + q - 2 >= 0) & (row + q - 2 < CELLS) & column_in
                    below[word, dj + 2, q] = jnp.where(good, turned_word, -1)

    def kept(table, dz, di, dj, spot, column_step):
        k = class_index(dz, di, dj)
        return jnp.bitwise_and(table[k // 30, column_step + 2, spot], 1 << (k % 30)) == 0

    def bonds(m, carry):
        x = [own[field, m] for field in range(12)]
        total = [force[field, m] for field in range(12)]
        for di, dj in PLANE:
            spot = m + 2 + di
            radius = di * di + dj * dj
            y = [moved[dj + 2, slot, spot] if slot != 6 else None for slot in range(13)]
            weight = [0.0] + [INTER_C * RATE / float(dz * dz + radius) ** 1.5 for dz in (1, 2, 3)]
            first = kept(words, 1, di, dj, spot, dj)
            far0, far1 = along(di, dj, y[0], y[1]), along(di, dj, y[3], y[4])
            near3, near2 = along(di, dj, x[9], x[10]), along(di, dj, x[6], x[7])
            t = jnp.where(first, weight[1] * gap(far0, near3, 1, y[2], x[11]), 0.0)
            plane3, lift3 = t, t
            plane2 = None
            if radius <= 5:
                second = kept(words, 2, di, dj, spot, dj)
                t = jnp.where(second, weight[2] * gap(far1, near3, 2, y[5], x[11]), 0.0)
                plane3, lift3 = plane3 + t, lift3 + 2.0 * t
                plane2 = jnp.where(second, weight[2] * gap(far0, near2, 2, y[2], x[8]), 0.0)
            total[11] = total[11] + lift3
            if di:
                total[9] = total[9] + scaled(di, plane3)
            if dj:
                total[10] = total[10] + scaled(dj, plane3)
            if plane2 is not None:
                total[8] = total[8] + 2.0 * plane2
                if di:
                    total[6] = total[6] + scaled(di, plane2)
                if dj:
                    total[7] = total[7] + scaled(dj, plane2)
            first = kept(below, 1, -dj, -di, spot, dj)
            far3, far2 = along(di, dj, y[7], y[8]), along(di, dj, y[10], y[11])
            near0, near1 = along(di, dj, x[0], x[1]), along(di, dj, x[3], x[4])
            t = jnp.where(first, weight[1] * gap(far3, near0, -1, y[9], x[2]), 0.0)
            plane0, lift0 = t, t
            plane1 = None
            if radius <= 5:
                second = kept(below, 2, -dj, -di, spot, dj)
                t = jnp.where(second, weight[2] * gap(far2, near0, -2, y[12], x[2]), 0.0)
                plane0, lift0 = plane0 + t, lift0 + 2.0 * t
                plane1 = jnp.where(second, weight[2] * gap(far3, near1, -2, y[9], x[5]), 0.0)
            total[2] = total[2] - lift0
            if di:
                total[0] = total[0] + scaled(di, plane0)
            if dj:
                total[1] = total[1] + scaled(dj, plane0)
            if plane1 is not None:
                total[5] = total[5] - 2.0 * plane1
                if di:
                    total[3] = total[3] + scaled(di, plane1)
                if dj:
                    total[4] = total[4] + scaled(dj, plane1)
            if radius == 0:
                rise = 9.0 * weight[3]
                third = kept(words, 3, 0, 0, spot, 0)
                top = facing[spot, 48:56]
                total[11] = total[11] + jnp.where(third, rise * (top - x[11]), 0.0)
                total[8] = total[8] + jnp.where(third, rise * (y[5] - x[8]), 0.0)
                total[5] = total[5] + jnp.where(third, rise * (y[2] - x[5]), 0.0)
                third = kept(below, 3, 0, 0, spot, 0)
                bottom = facing[spot, 104:112]
                total[2] = total[2] + jnp.where(third, rise * (bottom - x[2]), 0.0)
                total[5] = total[5] + jnp.where(third, rise * (y[12] - x[5]), 0.0)
                total[8] = total[8] + jnp.where(third, rise * (y[9] - x[8]), 0.0)
        for field in range(12):
            shared[8 * field + m] = total[field]
            shared[8 * field + 4 + m] = total[field]
        return carry

    lax.fori_loop(0, 4, bonds, 0)
    flat = shared.reshape(96 * 8, 128)
    low_row = jnp.bitwise_and(lax.broadcasted_iota(I32, (TURNS, 96), 1), 7) < 4
    for position in range(8):
        both = flat[pl.ds(position, 96, stride=8), :].T
        turned[pl.ds(position, TURNS, stride=8), 0:96] = jnp.where(low_row, both[0:TURNS], both[TURNS:])
    top = (ply == (lax.axis_size("ply") if not INTERPRET else 8) - 1).astype(F32)
    for piece in range(4):
        columns = slice(128 * piece, 128 * piece + 128)
        back = turned[columns, :].T
        for layer in range(4):
            for comp in range(3):
                field = 3 * layer + comp
                value = back[8 * field : 8 * field + 8]
                if field == 11:
                    value = value - (IMPACT * top) * mask[:, columns].astype(F32)
                new_a[comp, 0, layer, :, columns] = value
                new_v[comp, 0, layer, :, columns] = half[comp, 0, layer, :, columns] + 0.5 * value


def shape(*dims, dtype=F32):
    return jax.ShapeDtypeStruct(dims, dtype)


def run_advance(displacement, velocity, acceleration, flags):
    return pl.pallas_call(
        advance_kernel,
        out_shape=(
            shape(3, 1, 4, ROWS, CELLS),
            shape(3, 1, 4, ROWS, CELLS),
            shape(56, CELLS),
            shape(64, CELLS),
            shape(12, 3, CELLS),
            shape(12, 3, CELLS),
        ),
        interpret=INTERPRET,
    )(displacement, velocity, acceleration, flags)


def run_turn(above, below):
    call = kernel_call(turn_kernel, shape(TURNS * WINDOW, 128), [pltpu.VMEM((CELLS + 16, 128), F32)], 1_000_000)
    return call(above, below)


def run_pair(adv, low, high, codes, flags):
    vmem = pl.BlockSpec(memory_space=pltpu.VMEM)
    return pl.pallas_call(
        pair_kernel,
        out_shape=(shape(12, 4, 8, 128), shape(12, 4, 8, 128), shape(2, 5, 8, 8, 128, dtype=I32)),
        in_specs=[vmem, vmem, vmem, pl.BlockSpec(memory_space=pltpu.SMEM), vmem],
        scratch_shapes=[
            pltpu.VMEM((2, 128, CELLS), F32),
            pltpu.VMEM((2, CELLS, 128), F32),
            pltpu.VMEM((8 * 128, 128), F32),
            pltpu.VMEM((5, 12, 10, 8, 128), F32),
            pltpu.VMEM((2, 4, 4, 8, 128), F32),
            pltpu.VMEM((26, 6, 8, 128), F32),
            pltpu.VMEM((7, 10, 8, 128), F32),
            pltpu.VMEM((8, 128), I32),
        ],
        interpret=INTERPRET,
        cost_estimate=pl.CostEstimate(flops=50_000_000, bytes_accessed=2_000_000, transcendentals=0),
    )(adv, low, high, codes, flags)


def run_interface(message, own, words, force, half, mask):
    return pl.pallas_call(
        interface_kernel,
        out_shape=(shape(3, 1, 4, ROWS, CELLS), shape(3, 1, 4, ROWS, CELLS)),
        scratch_shapes=[
            pltpu.VMEM((8, 128, 128), F32),
            pltpu.VMEM((5, 13, 8, 8, 128), F32),
            pltpu.VMEM((2, 5, 8, 8, 128), I32),
            pltpu.VMEM((96, 8, 128), F32),
            pltpu.VMEM((CELLS, 128), F32),
        ],
        interpret=INTERPRET,
    )(message, own, words, force, half, mask)


def steps(axis, by):
    count = lax.axis_size(axis)
    return [(i, i + by) for i in range(count) if 0 <= i + by < count]


def local(displacement, velocity, acceleration, fibre_codes, contact_mask, bond_flags):
    adv, half, down, up, low, high = run_advance(displacement, velocity, acceleration, bond_flags)
    above = lax.ppermute(down, "ply", steps("ply", -1))
    below = lax.ppermute(up, "ply", steps("ply", 1))
    low = lax.ppermute(low, "stripe", steps("stripe", 1))
    high = lax.ppermute(high, "stripe", steps("stripe", -1))
    message = run_turn(above, below).reshape(TURNS, 1, WINDOW * 128)
    message = lax.all_to_all(message, "stripe", 0, 0).reshape(TURNS * WINDOW, 128)
    force, own, words = run_pair(adv, low, high, fibre_codes, bond_flags)
    new_velocity, new_acceleration = run_interface(message, own, words, force, half, contact_mask)
    return adv, new_velocity, new_acceleration


def solution(mesh):
    state = P(None, "ply", None, "stripe", None)
    return jax.shard_map(
        local,
        mesh=mesh,
        in_specs=(state, state, state, P("ply", None), P("stripe", None), P("ply", None, "stripe", None)),
        out_specs=(state, state, state),
        check_vma=False,
    )
```

profile of v0, /device:TPU:23, one launch (start us, length us, event | category | flops | bytes accessed | tf_op | source)
XLA Modules:
  0.0 55.6 jit_solution(838542774272577962)
XLA Ops:
  0.6 2.1 %shard_map.85 = (f32[3,1,4,8,512]{4,3,2,1,0:T(8,128)}, f32[3,1,4,8,512]{4,3,2,1,0:T(8,128)}, f32[56,512]{1,0:T(8,128)}, f32[64,512]{1,0:T(8,128)}, f32[12,3,512]{2,1,0:T(4,128)}, /*index=5*/f32[12,3,512]{2,1,0:T(4,128)}) custom-call(f32[3,1,4,8,512]{4,3,2,1,0:T(8,128)} %disp.1, f32[3,1,4,8,512]{4,3,2,1,0:T(8,128)} %vel.1, f32[3,1,4,8,512]{4,3,2,1,0:T(8,128)} %acc.1, ...), custom_call_target="tpu_custom_call" | custom-call | tf_op jit(solution)/shard_map/pallas_call | solution.py:398
  2.7 3.1 %collective-permute-start.1 = (f32[64,512]{1,0:T(8,128)}, f32[64,512]{1,0:T(8,128)S(1)}, u32[]{:S(2)}, u32[]{:S(2)}) collective-permute-start(f32[64,512]{1,0:T(8,128)} %get-tuple-element.16), channel_id=1, source_target_pairs={{0,64},{64,128},{128,192},{192,256},{256,320},{320,384},{384,448},... | collective-permute-start | bytes 393224 | tf_op jit(solution)/shard_map/ppermute | solution.py:461
  5.8 2.2 %collective-permute-start = (f32[56,512]{1,0:T(8,128)}, f32[56,512]{1,0:T(8,128)S(1)}, u32[]{:S(2)}, u32[]{:S(2)}) collective-permute-start(f32[56,512]{1,0:T(8,128)} %get-tuple-element.15), channel_id=1, source_target_pairs={{64,0},{128,64},{192,128},{256,192},{320,256},{384,320},{448,384},... | collective-permute-start | bytes 344072 | tf_op jit(solution)/shard_map/ppermute | solution.py:460
  8.0 5.7 %collective-permute-done.above = f32[56,512]{1,0:T(8,128)S(1)} collective-permute-done((f32[56,512]{1,0:T(8,128)}, f32[56,512]{1,0:T(8,128)S(1)}, u32[]{:S(2)}, u32[]{:S(2)}) %collective-permute-start) | collective-permute-done | bytes 114720 | tf_op jit(solution)/shard_map/ppermute | solution.py:460
  13.7 0.0 collective-permute-done.1.below
  13.7 0.9 %shard_map.86 = f32[768,128]{1,0:T(8,128)} custom-call(f32[56,512]{1,0:T(8,128)S(1)} %collective-permute-done.above, f32[64,512]{1,0:T(8,128)S(1)} %collective-permute-done.1.below), custom_call_target="tpu_custom_call" | custom-call | flops 1000000 | bytes 2000000 | tf_op jit(solution)/shard_map/pallas_call | solution.py:414
  14.6 0.0 copy-start.4
  14.6 0.0 copy-start.3
  14.6 17.4 %all-to-all-start = ((f32[64,1,1536]{2,1,0:T(1,128)}), f32[64,1,1536]{2,1,0:T(1,128)S(1)}, u32[]{:S(2)}, u32[]{:S(2)}) async-start(f32[64,1,1536]{2,1,0:T(1,128)} %bitcast), calls=%async_computation | async-start | bytes 786432 | tf_op jit(solution)/shard_map/all_to_all | solution.py:465
  32.0 0.0 copy-done.4
  32.0 5.5 %collective-permute-start.2 = (f32[12,3,512]{2,1,0:T(4,128)S(1)}, f32[12,3,512]{2,1,0:T(4,128)S(1)}, u32[]{:S(2)}, u32[]{:S(2)}) collective-permute-start(f32[12,3,512]{2,1,0:T(4,128)S(1)} %copy-done.4), channel_id=1, source_target_pairs={{0,1},{1,2},{2,3},{3,4},{4,5},{5,6},{6,7},{7,8},{8,9},{9,10},{10,1... | collective-permute-start | bytes 221192 | tf_op jit(solution)/shard_map/ppermute | solution.py:462
  37.5 0.0 copy-done.3
  37.5 1.9 %collective-permute-start.3 = (f32[12,3,512]{2,1,0:T(4,128)S(1)}, f32[12,3,512]{2,1,0:T(4,128)S(1)}, u32[]{:S(2)}, u32[]{:S(2)}) collective-permute-start(f32[12,3,512]{2,1,0:T(4,128)S(1)} %copy-done.3), channel_id=1, source_target_pairs={{1,0},{2,1},{3,2},{4,3},{5,4},{6,5},{7,6},{8,7},{9,8},{10,9},{11,1... | collective-permute-start | bytes 221192 | tf_op jit(solution)/shard_map/ppermute | solution.py:463
  39.5 1.3 %collective-permute-done.2.low = f32[12,3,512]{2,1,0:T(4,128)S(1)} collective-permute-done((f32[12,3,512]{2,1,0:T(4,128)S(1)}, f32[12,3,512]{2,1,0:T(4,128)S(1)}, u32[]{:S(2)}, u32[]{:S(2)}) %collective-permute-start.2) | collective-permute-done | bytes 73760 | tf_op jit(solution)/shard_map/ppermute | solution.py:462
  40.8 0.0 copy-start.1
  40.8 5.1 %collective-permute-done.3.high = f32[12,3,512]{2,1,0:T(4,128)S(1)} collective-permute-done((f32[12,3,512]{2,1,0:T(4,128)S(1)}, f32[12,3,512]{2,1,0:T(4,128)S(1)}, u32[]{:S(2)}, u32[]{:S(2)}) %collective-permute-start.3) | collective-permute-done | bytes 73760 | tf_op jit(solution)/shard_map/ppermute | solution.py:463
  45.9 0.0 copy-start.2
  45.9 0.0 copy-done.1
  45.9 0.6 %copy-done.2 = f32[12,3,512]{2,1,0:T(4,128)} copy-done((f32[12,3,512]{2,1,0:T(4,128)}, f32[12,3,512]{2,1,0:T(4,128)S(1)}, u32[]{:S(2)}) %copy-start.2) | copy-done | bytes 73752
  46.5 4.5 %shard_map.87 = (f32[12,4,8,128]{3,2,1,0:T(8,128)}, f32[12,4,8,128]{3,2,1,0:T(8,128)}, s32[2,5,8,8,128]{4,3,2,1,0:T(8,128)}) custom-call(f32[3,1,4,8,512]{4,3,2,1,0:T(8,128)} %get-tuple-element.11.adv, f32[12,3,512]{2,1,0:T(4,128)} %copy-done.1, f32[12,3,512]{2,1,0:T(4,128)} %copy-done.2, s32[1,2]{1,0:T(1,128)} %codes.1, s32[1,2,1,64]{3,2,1,0:T(1,128)} %flags.3), custom_call_target="tpu_custom_call" | custom-call | flops 50000000 | bytes 2000000 | tf_op jit(solution)/shard_map/pallas_call | solution.py:419
  51.0 0.0 all-to-all-done
  51.0 0.0 copy-start
  51.0 0.7 %copy-done = f32[64,1,1536]{2,1,0:T(1,128)} copy-done((f32[64,1,1536]{2,1,0:T(1,128)}, f32[64,1,1536]{2,1,0:T(1,128)S(1)}, u32[]{:S(2)}) %copy-start) | copy-done | bytes 393240
  51.7 3.9 %shard_map.88 = (f32[3,1,4,8,512]{4,3,2,1,0:T(8,128)}, f32[3,1,4,8,512]{4,3,2,1,0:T(8,128)}) custom-call(f32[768,128]{1,0:T(8,128)} %bitcast.2, f32[12,4,8,128]{3,2,1,0:T(8,128)} %get-tuple-element.19.own, s32[2,5,8,8,128]{4,3,2,1,0:T(8,128)} %get-tuple-element.20.words, f32[12,4,8,128]{3,2,1,0:T(8,128)} %get-tuple-element.21.force, ...), custom_call_target="tpu_custom_call" | custom-call | tf_op jit(solution)/shard_map/pallas_call | solution.py:439
Async XLA Ops:
  2.7 11.0 %collective-permute-start.1 = (f32[64,512]{1,0:T(8,128)}, f32[64,512]{1,0:T(8,128)S(1)}, u32[]{:S(2)}, u32[]{:S(2)}) collective-permute-start(f32[64,512]{1,0:T(8,128)} %get-tuple-element.16), channel_id=1, source_target_pairs={{0,64},{64,128},{128,192},{192,256},{256,320},{320,384},{384,448},... | collective-permute-start | bytes 393224 | tf_op jit(solution)/shard_map/ppermute | solution.py:461
  5.8 7.9 %collective-permute-start = (f32[56,512]{1,0:T(8,128)}, f32[56,512]{1,0:T(8,128)S(1)}, u32[]{:S(2)}, u32[]{:S(2)}) collective-permute-start(f32[56,512]{1,0:T(8,128)} %get-tuple-element.15), channel_id=1, source_target_pairs={{64,0},{128,64},{192,128},{256,192},{320,256},{384,320},{448,384},... | collective-permute-start | bytes 344072 | tf_op jit(solution)/shard_map/ppermute | solution.py:460
  14.6 17.4 %copy-start.4 = (f32[12,3,512]{2,1,0:T(4,128)S(1)}, f32[12,3,512]{2,1,0:T(4,128)}, u32[]{:S(2)}) copy-start(f32[12,3,512]{2,1,0:T(4,128)} %get-tuple-element.17) | copy-start | bytes 221188
  14.6 22.9 %copy-start.3 = (f32[12,3,512]{2,1,0:T(4,128)S(1)}, f32[12,3,512]{2,1,0:T(4,128)}, u32[]{:S(2)}) copy-start(f32[12,3,512]{2,1,0:T(4,128)} %get-tuple-element.18) | copy-start | bytes 221188
  14.6 36.4 %all-to-all-start = ((f32[64,1,1536]{2,1,0:T(1,128)}), f32[64,1,1536]{2,1,0:T(1,128)S(1)}, u32[]{:S(2)}, u32[]{:S(2)}) async-start(f32[64,1,1536]{2,1,0:T(1,128)} %bitcast), calls=%async_computation | async-start | bytes 786432 | tf_op jit(solution)/shard_map/all_to_all | solution.py:465
  32.0 8.8 %collective-permute-start.2 = (f32[12,3,512]{2,1,0:T(4,128)S(1)}, f32[12,3,512]{2,1,0:T(4,128)S(1)}, u32[]{:S(2)}, u32[]{:S(2)}) collective-permute-start(f32[12,3,512]{2,1,0:T(4,128)S(1)} %copy-done.4), channel_id=1, source_target_pairs={{0,1},{1,2},{2,3},{3,4},{4,5},{5,6},{6,7},{7,8},{8,9},{9,10},{10,1... | collective-permute-start | bytes 221192 | tf_op jit(solution)/shard_map/ppermute | solution.py:462
  37.5 8.3 %collective-permute-start.3 = (f32[12,3,512]{2,1,0:T(4,128)S(1)}, f32[12,3,512]{2,1,0:T(4,128)S(1)}, u32[]{:S(2)}, u32[]{:S(2)}) collective-permute-start(f32[12,3,512]{2,1,0:T(4,128)S(1)} %copy-done.3), channel_id=1, source_target_pairs={{1,0},{2,1},{3,2},{4,3},{5,4},{6,5},{7,6},{8,7},{9,8},{10,9},{11,1... | collective-permute-start | bytes 221192 | tf_op jit(solution)/shard_map/ppermute | solution.py:463
  40.8 5.1 %copy-start.1 = (f32[12,3,512]{2,1,0:T(4,128)}, f32[12,3,512]{2,1,0:T(4,128)S(1)}, u32[]{:S(2)}) copy-start(f32[12,3,512]{2,1,0:T(4,128)S(1)} %collective-permute-done.2.low) | copy-start | bytes 221188
  45.9 0.6 %copy-start.2 = (f32[12,3,512]{2,1,0:T(4,128)}, f32[12,3,512]{2,1,0:T(4,128)S(1)}, u32[]{:S(2)}) copy-start(f32[12,3,512]{2,1,0:T(4,128)S(1)} %collective-permute-done.3.high) | copy-start | bytes 221188
  51.0 0.7 %copy-start = (f32[64,1,1536]{2,1,0:T(1,128)}, f32[64,1,1536]{2,1,0:T(1,128)S(1)}, u32[]{:S(2)}) copy-start(f32[64,1,1536]{2,1,0:T(1,128)S(1)} %all-to-all-done) | copy-start | bytes 1179652
where the time goes:
time: 56 us; the launch traced here: 55.6 us
  starting transfers between devices  30.1 us (54%)
  waiting for transfers between devices  12.1 us (22%)
  Pallas kernels  11.4 us (20%)
  local copies, waits for them, and re-layouts  1.39 us (2%)
  between operations  0.7 us (1%)
    all_to_all x1, starting transfers between devices, local(): lax.all_to_all(message, 'stripe', 0, 0).reshape(TURNS * WINDOW, 128)  17.4 us
    ppermute x1, waiting for transfers between devices, local(): above = lax.ppermute(down, 'ply', steps('ply', -1))  5.69 us
    ppermute x1, starting transfers between devices, local(): low = lax.ppermute(low, 'stripe', steps('stripe', 1))  5.48 us
    ppermute x1, waiting for transfers between devices, local(): high = lax.ppermute(high, 'stripe', steps('stripe', -1))  5.08 us
    pallas_call x1, Pallas kernels, run_pair(): pl.pallas_call(pair_kernel, out_shape=(shape(12, 4, 8, 128), shape(12, 4,...  4.47 us
    pallas_call x1, Pallas kernels, run_interface(): pl.pallas_call(interface_kernel, out_shape=(shape(3, 1, 4, ROWS, CELLS),...  3.91 us
    ppermute x1, starting transfers between devices, local(): below = lax.ppermute(up, 'ply', steps('ply', 1))  3.11 us
    ppermute x1, starting transfers between devices, local(): above = lax.ppermute(down, 'ply', steps('ply', -1))  2.16 us
  transfers between devices with their start and end apart: 5, of which 3 were waited for; matrix products, arithmetic and copies ran while one was open for 0% of the time, Pallas kernels for 8%

commit v1 on v0

v1 whole, which is shorter than its diff:
```python
import jax
import jax.numpy as jnp
from jax import lax
from jax.experimental import pallas as pl
from jax.experimental.pallas import tpu as pltpu
from jax.sharding import PartitionSpec as P


ROOT_HALF = 0.7071067811865476
RATE = 0.025
MATRIX_C = 1.0
FIBRE_C = 4.0
INTER_C = 1.5
IMPACT = 2.0

F32 = jnp.float32
I32 = jnp.int32
ROWS = 8
TURNS = 64
CELLS = ROWS * TURNS
WINDOW = 11
SPREAD = [(2, 0), (3, 16), (4, 32), (5, 56), (6, 72), (7, 88)]
PLANE = [(di, dj) for di in range(-2, 3) for dj in range(-2, 3)]
INTERPRET = False


def place():
    return lax.axis_index("ply"), lax.axis_index("stripe")


def class_index(dz, di, dj):
    count = 0
    for z in range(1, 4):
        for i in range(-3, 4):
            for j in range(-3, 4):
                if z * z + i * i + j * j <= 9:
                    if (z, i, j) == (dz, di, dj):
                        return count
                    count += 1
    raise ValueError("no class")


def scaled(factor, value):
    if factor == 1:
        return value
    if factor == -1:
        return -value
    return factor * value


def along(di, dj, first, second):
    if di == 0 and dj == 0:
        return None
    if di == 0:
        return scaled(dj, second)
    if dj == 0:
        return scaled(di, first)
    if abs(di) == abs(dj):
        inner = first + second if di == dj else first - second
        return scaled(di, inner)
    return scaled(di, first) + scaled(dj, second)


def gap(far, near, rise, far_z, near_z):
    total = None if far is None else far - near
    if rise:
        lift = scaled(rise, far_z - near_z)
        total = lift if total is None else total + lift
    return total


def added(total, value):
    return value if total is None else total + value


def lanes_and_cells():
    cell = lax.broadcasted_iota(I32, (8, 128), 0)
    lane = lax.broadcasted_iota(I32, (8, 128), 1)
    return cell, lane


def shifted_by(value, cell):
    after = pltpu.roll(value, 127, 1)
    before = pltpu.roll(value, 1, 1)
    moved = {}
    for dj in (1, 2):
        moved[dj] = pltpu.roll(jnp.where(cell < dj, after, value), 8 - dj, 0)
        moved[-dj] = pltpu.roll(jnp.where(cell >= 8 - dj, before, value), dj, 0)
    return moved, after, before


def advance_kernel(disp, vel, acc, flags, adv, half, down, up, low, high):
    values = []
    for layer in range(4):
        for comp in range(3):
            speed = vel[comp, 0, layer] + 0.5 * acc[comp, 0, layer]
            moved = disp[comp, 0, layer] + speed
            half[comp, 0, layer] = speed
            adv[comp, 0, layer] = moved
            field = 3 * layer + comp
            low[3 * field : 3 * field + 3] = moved[5:8]
            high[3 * field : 3 * field + 3] = moved[0:3]
            values.append(moved)
    low[36:40] = jnp.zeros((4, CELLS), F32)
    high[36:40] = jnp.zeros((4, CELLS), F32)
    for slot, field in enumerate((1, 0, 2, 4, 3, 5, 8)):
        down[8 * slot : 8 * slot + 8] = values[field]
    for slot, field in enumerate((10, 9, 11, 7, 6, 8, 5)):
        up[8 * slot : 8 * slot + 8] = values[field]
    first = flags[0, 0]
    second = flags[0, 1]
    parts = jnp.concatenate(
        [jnp.bitwise_and(first, 0x7FFF), jnp.right_shift(first, 15), second, jnp.zeros((5, TURNS), I32)],
        axis=0,
    ).astype(F32)
    block = lax.broadcasted_iota(I32, (TURNS, CELLS), 0)
    column = lax.broadcasted_iota(I32, (TURNS, CELLS), 1)
    spread = (jnp.right_shift(column, 3) == block).astype(F32)
    up[56:64] = jnp.dot(parts, spread, precision=lax.Precision.HIGHEST, preferred_element_type=F32)


def turn_kernel(above, below, message, turned):
    stacked = jnp.concatenate([above[...], below[...], jnp.zeros((8, CELLS), F32)], axis=0)
    turned[0:8] = jnp.zeros((8, 128), F32)
    turned[CELLS + 8 : CELLS + 16] = jnp.zeros((8, 128), F32)
    for piece in range(4):
        turned[8 + 128 * piece : 136 + 128 * piece] = stacked[:, 128 * piece : 128 * piece + 128].T
    lane = lax.broadcasted_iota(I32, (TURNS, 128), 1)
    last = turned[pl.ds(17, TURNS, stride=8), :]
    starts = dict(SPREAD)
    for row in range(WINDOW):
        line = turned[pl.ds(6 + row, TURNS, stride=8), :]
        if row in starts:
            line = jnp.where(lane < 112, line, pltpu.roll(last, 112 - starts[row], 1))
        message[pl.ds(row, TURNS, stride=WINDOW), :] = line


def coefficient(here, there, dz, di, dj):
    radius = float(dz * dz + di * di + dj * dj)
    level = RATE / radius**1.5
    return level * MATRIX_C + (level * FIBRE_C * 0.5 / radius) * (here + there)


def pair_bonds(di, dj, x, y, here, rate, total):
    far_e = [along(di, dj, y[3 * l], y[3 * l + 1]) for l in range(4)]
    near_e = [along(di, dj, x[3 * l], x[3 * l + 1]) for l in range(4)]
    for layer in range(4):
        plane, lift = None, None
        for other in range(4):
            dz = other - layer
            if dz * dz + di * di + dj * dj > 9 or (dz, di, dj) == (0, 0, 0) or abs(dz) == 3:
                continue
            pick = (layer // 2, 2 + min(layer, other), 5)[abs(dz)]
            s = gap(far_e[other], near_e[layer], dz, y[3 * other + 2], x[3 * layer + 2])
            t = rate(pick) * s
            plane = added(plane, t)
            if abs(dz) == 1:
                lift = added(lift, t if dz > 0 else -t)
            if abs(dz) == 2:
                lift = added(lift, scaled(dz, t))
        if di or dj:
            plane = plane * here
            if di:
                total[3 * layer] = added(total[3 * layer], scaled(di, plane))
            if dj:
                total[3 * layer + 1] = added(total[3 * layer + 1], scaled(dj, plane))
        total[3 * layer + 2] = added(total[3 * layer + 2], lift * here)


def pair_kernel(adv, codes, flags, mask, force, base, strengths, rates, present, impact, turned, held, moved, far, spare):
    ply, stripe = place()
    cell, lane = lanes_and_cells()
    for side in range(2):
        rows = []
        for field in range(12):
            whole = adv[field % 3, 0, field // 3]
            rows.append(whole if side == 0 else pltpu.roll(whole, 4, 0))
        stacked = jnp.concatenate(rows, axis=0)
        for piece in range(4):
            turned[side, 128 * piece : 128 * piece + 128, 0:96] = stacked[:, 128 * piece : 128 * piece + 128].T
    for position in range(8):
        pick = pl.ds(position, TURNS, stride=8)
        both = jnp.concatenate([turned[0, pick, :], turned[1, pick, :]], axis=0)
        held[96 * position : 96 * position + 96] = both.T[0:96]
    for field in range(12):
        for q in range(8):
            value = held[pl.ds(8 * field + q, 8, stride=96), :]
            base[field, q] = value
            if q < 4:
                others, after, before = shifted_by(value, cell)
                for dj, other in others.items():
                    moved[dj + 2, field, q] = other
                if field % 3 == 1:
                    far[0, field // 3, q] = pltpu.roll(jnp.where(cell >= 5, before, value), 3, 0)
                    far[1, field // 3, q] = pltpu.roll(jnp.where(cell < 3, after, value), 5, 0)
    row = 8 * stripe + jnp.where(lane >= TURNS, 4, 0)
    column = 8 * jnp.bitwise_and(lane, TURNS - 1) + cell
    row_in = [(row + q >= 0) & (row + q < CELLS) for q in range(-3, 7)]
    for dj in range(-3, 4):
        column_in = (column + dj >= 0) & (column + dj < CELLS)
        for q in range(-3, 7):
            present[dj + 3, q + 3] = (row_in[q + 3] & column_in).astype(F32)
    spare[0:1, 0:TURNS] = flags[0, 0]
    spare[1:2, 0:TURNS] = flags[0, 1]
    both = spare[...]
    both = jnp.where(lane < TURNS, both, pltpu.roll(both, TURNS, 1))
    plain = [jnp.broadcast_to(both[word : word + 1], (8, 128)) for word in range(2)]
    top = ply == (lax.axis_size("ply") if not INTERPRET else 8) - 1
    lower = jnp.where(top, 0.0, 1.0)
    for spot, (di, dj) in enumerate(PLANE):
        for dz in (1, 2, 3):
            if dz * dz + di * di + dj * dj <= 9:
                k = class_index(dz, di, dj)
                whole = jnp.bitwise_and(plain[k // 30], 1 << (k % 30)) == 0
                strength = jnp.where(whole, lower * weight(dz, di, dj), 0.0)
                for m in range(4):
                    strengths[dz - 1 if dz < 3 else 0, spot if dz < 3 else 25, m] = strength * present[dj + 3, m + di + 3]
    impact[...] = (IMPACT * top.astype(F32)) * mask[...].astype(F32)
    cos_parts, sin_parts = [], []
    for side in range(2):
        code = codes[0, side]
        cosine = jnp.where(code == 0, 1.0, jnp.where(code == 1, 0.0, ROOT_HALF))
        sine = jnp.where(code == 0, 0.0, jnp.where(code == 1, 1.0, jnp.where(code == 2, ROOT_HALF, -ROOT_HALF)))
        cos_parts.append(jnp.full((8, 128), cosine, F32))
        sin_parts.append(jnp.full((8, 128), sine, F32))
    for spot, (di, dj) in enumerate(PLANE):
        lean = [(di * cos_parts[side] + dj * sin_parts[side]) ** 2 for side in range(2)]
        if (di, dj) != (0, 0):
            rates[spot, 0] = coefficient(lean[0], lean[0], 0, di, dj)
            rates[spot, 1] = coefficient(lean[1], lean[1], 0, di, dj)
        rates[spot, 2] = coefficient(lean[0], lean[0], 1, di, dj)
        rates[spot, 3] = coefficient(lean[0], lean[1], 1, di, dj)
        rates[spot, 4] = coefficient(lean[1], lean[1], 1, di, dj)
        rates[spot, 5] = coefficient(lean[0], lean[1], 2, di, dj)
    for side in range(2):
        lean = (3 * cos_parts[side]) ** 2
        rates[25, side] = 9.0 * coefficient(lean, lean, 0, 3, 0)
        lean = (3 * sin_parts[side]) ** 2
        rates[25, 2 + side] = 9.0 * coefficient(lean, lean, 0, 0, 3)
    rates[25, 4] = 9.0 * coefficient(jnp.zeros((8, 128), F32), 0.0, 3, 0, 0)
    for m in range(4):
        x = [base[field, m] for field in range(12)]
        rise = rates[25, 4] * (x[11] - x[2])
        total = [None] * 12
        total[2], total[11] = rise, -rise
        for spot, (di, dj) in enumerate(PLANE):
            q = m + di
            if 0 <= q < 4:
                y = [moved[dj + 2, field, q] if dj else base[field, q] for field in range(12)]
                pair_bonds(di, dj, x, y, present[dj + 3, q + 3], lambda pick: rates[spot, pick], total)
        for layer in range(4):
            for step in (-3, 3):
                if 0 <= m + step < 4:
                    apart = base[3 * layer, m + step] - x[3 * layer]
                    total[3 * layer] = added(total[3 * layer], rates[25, layer // 2] * apart)
            for side, step in ((0, -3), (1, 3)):
                apart = present[3 + step, m + 3] * (far[side, layer, m] - x[3 * layer + 1])
                total[3 * layer + 1] = total[3 * layer + 1] + rates[25, 2 + layer // 2] * apart
        for field in range(12):
            force[field, m] = total[field]


def weight(dz, di, dj):
    return INTER_C * RATE / float(dz * dz + di * di + dj * dj) ** 1.5


EDGE_ROWS = (-2, -1, 4, 5)


def edge_kernel(low, high, base, rates, present, partial, force, turned, held, moved):
    cell, lane = lanes_and_cells()
    left = lane < TURNS
    for side, rows in enumerate((low, high)):
        for piece in range(4):
            turned[side, 128 * piece : 128 * piece + 128, 0:40] = rows[:, 128 * piece : 128 * piece + 128].T
    for position in range(8):
        pick = pl.ds(position, TURNS, stride=8)
        both = jnp.concatenate([turned[0, pick, :], turned[1, pick, :]], axis=0)
        held[40 * position : 40 * position + 40] = both.T[0:40]

    def around(field, q):
        other = held[pl.ds(3 * field + (q + 3 if q < 0 else q - 4), 8, stride=40), :]
        return jnp.where(left, other, base[field, q + 8]) if q < 0 else jnp.where(left, base[field, q], other)

    for field in range(12):
        for spot, q in enumerate(EDGE_ROWS):
            value = around(field, q)
            moved[2, field, spot] = value
            for dj, other in shifted_by(value, cell)[0].items():
                moved[dj + 2, field, spot] = other
    for m in range(4):
        x = [base[field, m] for field in range(12)]
        total = [partial[field, m] for field in range(12)]
        for spot, (di, dj) in enumerate(PLANE):
            q = m + di
            if q in EDGE_ROWS:
                y = [moved[dj + 2, field, EDGE_ROWS.index(q)] for field in range(12)]
                pair_bonds(di, dj, x, y, present[dj + 3, q + 3], lambda pick: rates[spot, pick], total)
        for layer in range(4):
            for q in (m - 3, m + 3):
                if q < 0 or q > 3:
                    apart = present[3, q + 3] * (around(3 * layer, q) - x[3 * layer])
                    total[3 * layer] = total[3 * layer] + rates[25, layer // 2] * apart
        for field in range(12):
            force[field, m] = total[field]


def grown(sums, key, sign, value):
    if key not in sums:
        sums[key] = value if sign > 0 else -value
    else:
        sums[key] = sums[key] + value if sign > 0 else sums[key] - value


def stretched(turn, far, near, rise, far_z, near_z):
    lift = far_z - near_z
    if abs(rise) == 2:
        lift = lift + lift
    if far is None:
        return lift, 1 if rise > 0 else -1
    core = far - near
    if rise > 0:
        return (core + lift if turn > 0 else lift - core), 1
    return (core - lift, 1) if turn > 0 else (core + lift, -1)


def pushed(sums, wide, field, di, dj, sign, value):
    for step, spot in ((di, field), (dj, field + 1)):
        if step:
            grown(sums if abs(step) == 1 else wide, spot, sign if step > 0 else -sign, value)


def interface_kernel(message, own, strengths, force, half, impact, new_v, new_a, facing, moved, below, shared, turned):
    ply, stripe = place()
    cell, lane = lanes_and_cells()
    wide_lane = lax.broadcasted_iota(I32, (TURNS, 128), 1)
    lines = [message[pl.ds(row, TURNS, stride=WINDOW), :] for row in range(WINDOW)]
    last = lines[0]
    for row, start in SPREAD:
        last = jnp.where(wide_lane < start, last, pltpu.roll(lines[row], start + 16, 1))
    lines.append(last)
    for q in range(8):
        facing[q] = jnp.concatenate([lines[q], lines[q + 4]], axis=0).T
    row = 8 * stripe + jnp.where(lane >= TURNS, 4, 0)
    column = 8 * jnp.bitwise_and(lane, TURNS - 1) + cell
    left = lane < TURNS
    same = facing[4, 112:120]
    twin = pltpu.roll(same, TURNS, 1)
    for parts, spots in (
        (jnp.where(left, facing[0, 112:120], same), (0, 1)),
        (jnp.where(left, twin, same), (2, 3, 4, 5)),
        (jnp.where(left, twin, facing[6, 112:120]), (6, 7)),
    ):
        parts = parts.astype(I32)
        joined = [jnp.bitwise_or(jnp.left_shift(parts[1:2], 15), parts[0:1]), parts[2:3]]
        for word in range(2):
            plain = jnp.broadcast_to(joined[word], (8, 128))
            before, after = pltpu.roll(plain, 1, 1), pltpu.roll(plain, 127, 1)
            for dj in range(-2, 3):
                turned_word = plain
                if dj < 0:
                    turned_word = jnp.where(cell + dj < 0, before, plain)
                if dj > 0:
                    turned_word = jnp.where(cell + dj > 7, after, plain)
                column_in = (column + dj >= 0) & (column + dj < CELLS) & (ply > 0)
                for q in spots:
                    good = (row + q - 2 >= 0) & (row + q - 2 < CELLS) & column_in
                    below[word, dj + 2, q] = jnp.where(good, turned_word, -1)

    def spread(q):
        for slot in (0, 1, 2, 3, 4, 5, 7, 8, 9, 10, 11, 12):
            field = facing[q, 8 * slot : 8 * slot + 8]
            for dj, other in shifted_by(field, cell)[0].items():
                moved[dj + 2, slot, q] = other

    def kept(dz, di, dj, spot, value):
        k = class_index(dz, -dj, -di)
        whole = jnp.bitwise_and(below[k // 30, dj + 2, spot], 1 << (k % 30)) == 0
        return jnp.where(whole, weight(dz, di, dj) * value, 0.0)

    def bonds(m):
        x = [own[field, m] for field in range(12)]
        sums = {field: force[field, m] for field in range(12)}
        wide, double = {}, {}
        for spot, (di, dj) in enumerate(PLANE):
            q = m + 2 + di
            close = di * di + dj * dj <= 5
            turn = 1 if (di, dj) >= (0, 0) else -1
            pi, pj = turn * di, turn * dj

            def y(slot):
                return moved[dj + 2, slot, q] if dj else facing[q, 8 * slot : 8 * slot + 8]

            far, far_z = along(pi, pj, y(0), y(1)), y(2)
            near = along(pi, pj, x[9], x[10])
            value, sign = stretched(turn, far, near, 1, far_z, x[11])
            first = strengths[0, spot, m] * value
            grown(sums, 11, sign, first)
            plane = first
            if close:
                value, sign = stretched(turn, along(pi, pj, y(3), y(4)), near, 2, y(5), x[11])
                second = strengths[1, spot, m] * value
                grown(double, 11, sign, second)
                plane = first + second
                value, sign = stretched(turn, far, along(pi, pj, x[6], x[7]), 2, far_z, x[8])
                second = strengths[1, spot, m] * value
                grown(double, 8, sign, second)
                pushed(sums, wide, 6, di, dj, sign, second)
            pushed(sums, wide, 9, di, dj, sign, plane)
            far, far_z = along(pi, pj, y(7), y(8)), y(9)
            near = along(pi, pj, x[0], x[1])
            value, sign = stretched(turn, far, near, -1, far_z, x[2])
            first = kept(1, di, dj, q, value)
            grown(sums, 2, -sign, first)
            plane = first
            if close:
                value, sign = stretched(turn, along(pi, pj, y(10), y(11)), near, -2, y(12), x[2])
                second = kept(2, di, dj, q, value)
                grown(double, 2, -sign, second)
                plane = first + second
                value, sign = stretched(turn, far, along(pi, pj, x[3], x[4]), -2, far_z, x[5])
                second = kept(2, di, dj, q, value)
                grown(double, 5, -sign, second)
                pushed(sums, wide, 3, di, dj, sign, second)
            pushed(sums, wide, 0, di, dj, sign, plane)
            if di == 0 and dj == 0:
                rise = 9.0 * strengths[0, 25, m]
                grown(sums, 11, 1, rise * (facing[q, 48:56] - x[11]))
                grown(sums, 8, 1, rise * (y(5) - x[8]))
                grown(sums, 5, 1, rise * (y(2) - x[5]))
                grown(sums, 2, 1, kept(3, 0, 0, q, 9.0 * (facing[q, 104:112] - x[2])))
                grown(sums, 5, 1, kept(3, 0, 0, q, 9.0 * (y(12) - x[5])))
                grown(sums, 8, 1, kept(3, 0, 0, q, 9.0 * (y(9) - x[8])))
        for extra in (wide, double):
            for field, value in extra.items():
                sums[field] = sums[field] + 2.0 * value
        for field in range(12):
            shared[8 * field + m] = sums[field]
            shared[8 * field + 4 + m] = sums[field]

    for q in range(4):
        spread(q)
    for m in range(4):
        spread(m + 4)
        bonds(m)
    flat = shared.reshape(96 * 8, 128)
    low_row = jnp.bitwise_and(lax.broadcasted_iota(I32, (TURNS, 96), 1), 7) < 4
    for position in range(8):
        both = flat[pl.ds(position, 96, stride=8), :].T
        turned[pl.ds(position, TURNS, stride=8), 0:96] = jnp.where(low_row, both[0:TURNS], both[TURNS:])
    for piece in range(4):
        columns = slice(128 * piece, 128 * piece + 128)
        back = turned[columns, :].T
        for layer in range(4):
            for comp in range(3):
                field = 3 * layer + comp
                value = back[8 * field : 8 * field + 8]
                if field == 11:
                    value = value - impact[:, columns]
                new_a[comp, 0, layer, :, columns] = value
                new_v[comp, 0, layer, :, columns] = half[comp, 0, layer, :, columns] + 0.5 * value


def shape(*dims, dtype=F32):
    return jax.ShapeDtypeStruct(dims, dtype)


def near(*dims, dtype=F32):
    return shape(*dims, dtype=dtype) if INTERPRET else pltpu.VMEM(dims, dtype)


def kept_near(array):
    return array if INTERPRET else pltpu.with_memory_space_constraint(array, pltpu.VMEM)


def run_advance(displacement, velocity, acceleration, flags):
    return pl.pallas_call(
        advance_kernel,
        out_shape=(
            near(3, 1, 4, ROWS, CELLS),
            near(3, 1, 4, ROWS, CELLS),
            near(56, CELLS),
            near(64, CELLS),
            near(40, CELLS),
            near(40, CELLS),
        ),
        interpret=INTERPRET,
    )(displacement, velocity, acceleration, flags)


def run_turn(above, below):
    return pl.pallas_call(
        turn_kernel,
        out_shape=near(TURNS * WINDOW, 128),
        scratch_shapes=[pltpu.VMEM((CELLS + 16, 128), F32)],
        interpret=INTERPRET,
        compiler_params=pltpu.CompilerParams(vmem_limit_bytes=16 * 1024 * 1024),
    )(kept_near(above), kept_near(below))


def run_pair(adv, codes, flags, mask):
    vmem = pl.BlockSpec(memory_space=pltpu.VMEM)
    return pl.pallas_call(
        pair_kernel,
        out_shape=(
            near(12, 4, 8, 128),
            near(12, 8, 8, 128),
            near(2, 26, 4, 8, 128),
            near(26, 6, 8, 128),
            near(7, 10, 8, 128),
            near(8, CELLS),
        ),
        in_specs=[vmem, pl.BlockSpec(memory_space=pltpu.SMEM), vmem, vmem],
        scratch_shapes=[
            pltpu.VMEM((2, CELLS, 128), F32),
            pltpu.VMEM((8 * 96, 128), F32),
            pltpu.VMEM((5, 12, 4, 8, 128), F32),
            pltpu.VMEM((2, 4, 4, 8, 128), F32),
            pltpu.VMEM((8, 128), I32),
        ],
        interpret=INTERPRET,
        compiler_params=pltpu.CompilerParams(vmem_limit_bytes=16 * 1024 * 1024),
        cost_estimate=pl.CostEstimate(flops=20_000_000, bytes_accessed=1_000_000, transcendentals=0),
    )(kept_near(adv), codes, flags, mask)


def run_edge(low, high, base, rates, present, partial):
    return pl.pallas_call(
        edge_kernel,
        out_shape=near(12, 4, 8, 128),
        scratch_shapes=[
            pltpu.VMEM((2, CELLS, 128), F32),
            pltpu.VMEM((8 * 40, 128), F32),
            pltpu.VMEM((5, 12, 4, 8, 128), F32),
        ],
        interpret=INTERPRET,
        compiler_params=pltpu.CompilerParams(vmem_limit_bytes=16 * 1024 * 1024),
        cost_estimate=pl.CostEstimate(flops=10_000_000, bytes_accessed=1_000_000, transcendentals=0),
    )(*[kept_near(array) for array in (low, high, base, rates, present, partial)])


def run_interface(message, own, strengths, force, half, impact):
    return pl.pallas_call(
        interface_kernel,
        out_shape=(shape(3, 1, 4, ROWS, CELLS), shape(3, 1, 4, ROWS, CELLS)),
        scratch_shapes=[
            pltpu.VMEM((8, 128, 128), F32),
            pltpu.VMEM((5, 13, 8, 8, 128), F32),
            pltpu.VMEM((2, 5, 8, 8, 128), I32),
            pltpu.VMEM((96, 8, 128), F32),
            pltpu.VMEM((CELLS, 128), F32),
        ],
        interpret=INTERPRET,
        compiler_params=pltpu.CompilerParams(vmem_limit_bytes=16 * 1024 * 1024),
    )(kept_near(message), kept_near(own), kept_near(strengths), kept_near(force), kept_near(half), kept_near(impact))


def steps(axis, by):
    count = lax.axis_size(axis)
    return [(i, i + by) for i in range(count) if 0 <= i + by < count]


def local(displacement, velocity, acceleration, fibre_codes, contact_mask, bond_flags):
    adv, half, down, up, low, high = run_advance(displacement, velocity, acceleration, bond_flags)
    above = lax.ppermute(down, "ply", steps("ply", -1))
    below = lax.ppermute(up, "ply", steps("ply", 1))
    low = lax.ppermute(low, "stripe", steps("stripe", 1))
    high = lax.ppermute(high, "stripe", steps("stripe", -1))
    message = run_turn(above, below).reshape(TURNS, 1, WINDOW * 128)
    message = lax.all_to_all(message, "stripe", 0, 0)
    partial, own, strengths, rates, present, impact = run_pair(adv, fibre_codes, bond_flags, contact_mask)
    force = run_edge(low, high, own, rates, present, partial)
    message = message.reshape(TURNS * WINDOW, 128)
    new_velocity, new_acceleration = run_interface(message, own, strengths, force, half, impact)
    return adv, new_velocity, new_acceleration


def solution(mesh):
    state = P(None, "ply", None, "stripe", None)
    return jax.shard_map(
        local,
        mesh=mesh,
        in_specs=(state, state, state, P("ply", None), P("stripe", None), P("ply", None, "stripe", None)),
        out_specs=(state, state, state),
        check_vma=False,
    )
```

time: 56 us -> 50.9 us (0.909)
  the two profiles are of different devices: /device:TPU:23 before, /device:TPU:1 now
where the time goes in v1:
time: 50.9 us; the launch traced here: 50.5 us
  starting transfers between devices  29.8 us (59%)
  waiting for transfers between devices  11.2 us (22%)
  Pallas kernels  8.12 us (16%)
  between operations  0.72 us (1%)
  local copies, waits for them, and re-layouts  0.7 us (1%)
    all_to_all x1, starting transfers between devices, local(): message = lax.all_to_all(message, 'stripe', 0, 0)  18.2 us
    ppermute x1, starting transfers between devices, local(): low = lax.ppermute(low, 'stripe', steps('stripe', 1))  4.44 us
    ppermute x1, waiting for transfers between devices, local(): above = lax.ppermute(down, 'ply', steps('ply', -1))  4.24 us
    ppermute x1, starting transfers between devices, local(): below = lax.ppermute(up, 'ply', steps('ply', 1))  3.94 us
    all_to_all x1, waiting for transfers between devices, local(): message = lax.all_to_all(message, 'stripe', 0, 0)  3.65 us
    ppermute x1, waiting for transfers between devices, local(): high = lax.ppermute(high, 'stripe', steps('stripe', -1))  3.28 us
    pallas_call x1, Pallas kernels, run_pair(): pl.pallas_call(pair_kernel, out_shape=(near(12, 4, 8, 128), near(12, 8, 8...  2.5 us
    pallas_call x1, Pallas kernels, run_interface(): pl.pallas_call(interface_kernel, out_shape=(shape(3, 1, 4, ROWS, CELLS),...  2.25 us
  transfers between devices with their start and end apart: 5, of which 3 were waited for; matrix products, arithmetic and copies ran while one was open for 1% of the time, Pallas kernels for 7%

profile of v1, /device:TPU:1, one launch (start us, length us, event | category | flops | bytes accessed | tf_op | source)
XLA Modules:
  0.0 50.5 jit_solution(2341412501466445238)
XLA Ops:
  0.6 1.4 %shard_map.85 = (f32[3,1,4,8,512]{4,3,2,1,0:T(8,128)S(1)}, f32[3,1,4,8,512]{4,3,2,1,0:T(8,128)S(1)}, f32[56,512]{1,0:T(8,128)S(1)}, f32[64,512]{1,0:T(8,128)S(1)...) custom-call(f32[3,1,4,8,512]{4,3,2,1,0:T(8,128)} %disp.1, f32[3,1,4,8,512]{4,3,2,1,0:T(8,128)} %vel.1, ...), custom_call_target="tpu_custom_call" | custom-call | tf_op jit(solution)/shard_map/pallas_call | solution.py:477
  2.0 3.9 %collective-permute-start.1 = (f32[64,512]{1,0:T(8,128)S(1)}, f32[64,512]{1,0:T(8,128)S(1)}, u32[]{:S(2)}, u32[]{:S(2)}) collective-permute-start(f32[64,512]{1,0:T(8,128)S(1)} %get-tuple-element.19), channel_id=1, source_target_pairs={{0,64},{64,128},{128,192},{192,256},{256,320},{320,384},{384,448},... | collective-permute-start | bytes 393224 | tf_op jit(solution)/shard_map/ppermute | solution.py:566
  5.9 1.3 %collective-permute-start = (f32[56,512]{1,0:T(8,128)S(1)}, f32[56,512]{1,0:T(8,128)S(1)}, u32[]{:S(2)}, u32[]{:S(2)}) collective-permute-start(f32[56,512]{1,0:T(8,128)S(1)} %get-tuple-element.18), channel_id=1, source_target_pairs={{64,0},{128,64},{192,128},{256,192},{320,256},{384,320},{448,384},... | collective-permute-start | bytes 344072 | tf_op jit(solution)/shard_map/ppermute | solution.py:565
  7.2 4.2 %collective-permute-done.above = f32[56,512]{1,0:T(8,128)S(1)} collective-permute-done((f32[56,512]{1,0:T(8,128)S(1)}, f32[56,512]{1,0:T(8,128)S(1)}, u32[]{:S(2)}, u32[]{:S(2)}) %collective-permute-start) | collective-permute-done | bytes 114720 | tf_op jit(solution)/shard_map/ppermute | solution.py:565
  11.5 0.0 collective-permute-done.1.below
  11.5 1.0 %shard_map.86 = f32[704,128]{1,0:T(8,128)} custom-call(f32[56,512]{1,0:T(8,128)S(1)} %collective-permute-done.above, f32[64,512]{1,0:T(8,128)S(1)} %collective-permute-done.1.below), custom_call_target="tpu_custom_call" | custom-call | tf_op jit(solution)/shard_map/pallas_call | solution.py:492
  12.5 18.2 %all-to-all-start = ((f32[64,1,1408]{2,1,0:T(1,128)}), f32[64,1,1408]{2,1,0:T(1,128)S(1)}, u32[]{:S(2)}, u32[]{:S(2)}) async-start(f32[64,1,1408]{2,1,0:T(1,128)} %bitcast), calls=%async_computation | async-start | bytes 720896 | tf_op jit(solution)/shard_map/all_to_all | solution.py:570
  30.7 4.4 %collective-permute-start.2 = (f32[40,512]{1,0:T(8,128)S(1)}, f32[40,512]{1,0:T(8,128)S(1)}, u32[]{:S(2)}, u32[]{:S(2)}) collective-permute-start(f32[40,512]{1,0:T(8,128)S(1)} %get-tuple-element.22), channel_id=1, source_target_pairs={{0,1},{1,2},{2,3},{3,4},{4,5},{5,6},{6,7},{7,8},{8,9},{9,10},{10,1... | collective-permute-start | bytes 245768 | tf_op jit(solution)/shard_map/ppermute | solution.py:567
  35.2 1.9 %collective-permute-start.3 = (f32[40,512]{1,0:T(8,128)S(1)}, f32[40,512]{1,0:T(8,128)S(1)}, u32[]{:S(2)}, u32[]{:S(2)}) collective-permute-start(f32[40,512]{1,0:T(8,128)S(1)} %get-tuple-element.23), channel_id=1, source_target_pairs={{1,0},{2,1},{3,2},{4,3},{5,4},{6,5},{7,6},{8,7},{9,8},{10,9},{11,1... | collective-permute-start | bytes 245768 | tf_op jit(solution)/shard_map/ppermute | solution.py:568
  37.1 0.0 copy-start
  37.1 0.0 copy-start.1
  37.1 0.0 copy-start.2
  37.1 0.7 %copy.10 = f32[3,1,4,8,512]{4,3,2,1,0:T(8,128)} copy(f32[3,1,4,8,512]{4,3,2,1,0:T(8,128)S(1)} %get-tuple-element.31.adv) | data formatting | bytes 393216
  37.8 0.0 copy-done
  37.8 0.0 copy-done.1
  37.8 0.0 copy-done.2
  37.8 2.5 %shard_map.87 = (f32[12,4,8,128]{3,2,1,0:T(8,128)S(1)}, f32[12,8,8,128]{3,2,1,0:T(8,128)S(1)}, f32[2,26,4,8,128]{4,3,2,1,0:T(8,128)S(1)}, f32[26,6,8,128]{3,2,1,...) custom-call(f32[3,1,4,8,512]{4,3,2,1,0:T(8,128)S(1)} %get-tuple-element.31.adv, ...), custom_call_target="tpu_custom_call" | custom-call | flops 20000000 | bytes 1000000 | tf_op jit(solution)/shard_map/pallas_call | solution.py:503
  40.3 0.0 collective-permute-done.2.low
  40.3 3.3 %collective-permute-done.3.high = f32[40,512]{1,0:T(8,128)S(1)} collective-permute-done((f32[40,512]{1,0:T(8,128)S(1)}, f32[40,512]{1,0:T(8,128)S(1)}, u32[]{:S(2)}, u32[]{:S(2)}) %collective-permute-start.3) | collective-permute-done | bytes 81952 | tf_op jit(solution)/shard_map/ppermute | solution.py:568
  43.6 1.0 %shard_map.88.force = f32[12,4,8,128]{3,2,1,0:T(8,128)S(1)} custom-call(f32[40,512]{1,0:T(8,128)S(1)} %collective-permute-done.2.low, f32[40,512]{1,0:T(8,128)S(1)} %collective-permute-done.3.high, f32[12,8,8,128]{3,2,1,0:T(8,128)S(1)} %get-tuple-element.20.base.own, f32[26,6,8,128]{3,2,1,0:T(8,128)S(1)} %get-tuple-element.24.rates, ...), custom_call_target="tpu_custom_call" | custom-call | flops 10000000 | bytes 1000000 | tf_op jit(solution)/shard_map/pallas_call | solution.py:528
  44.6 3.6 %all-to-all-done = f32[64,1,1408]{2,1,0:T(1,128)S(1)} async-done(((f32[64,1,1408]{2,1,0:T(1,128)}), f32[64,1,1408]{2,1,0:T(1,128)S(1)}, u32[]{:S(2)}, u32[]{:S(2)}) %all-to-all-start) | async-done | bytes 360480 | tf_op jit(solution)/shard_map/all_to_all | solution.py:570
  48.3 2.2 %shard_map.89 = (f32[3,1,4,8,512]{4,3,2,1,0:T(8,128)}, f32[3,1,4,8,512]{4,3,2,1,0:T(8,128)}) custom-call(f32[704,128]{1,0:T(8,128)S(1)} %bitcast.2, f32[12,8,8,128]{3,2,1,0:T(8,128)S(1)} %get-tuple-element.20.base.own, f32[2,26,4,8,128]{4,3,2,1,0:T(8,128)S(1)} %get-tuple-element.21.strengths, f32[12,4,8,128]{3,2,1,0:T(8,128)S(1)} %shard_map.88.force, ...), custom_call_target="tpu_custom_call" | custom-call | tf_op jit(solution)/shard_map/pallas_call | solution.py:543
Async XLA Ops:
  2.0 9.5 %collective-permute-start.1 = (f32[64,512]{1,0:T(8,128)S(1)}, f32[64,512]{1,0:T(8,128)S(1)}, u32[]{:S(2)}, u32[]{:S(2)}) collective-permute-start(f32[64,512]{1,0:T(8,128)S(1)} %get-tuple-element.19), channel_id=1, source_target_pairs={{0,64},{64,128},{128,192},{192,256},{256,320},{320,384},{384,448},... | collective-permute-start | bytes 393224 | tf_op jit(solution)/shard_map/ppermute | solution.py:566
  5.9 5.5 %collective-permute-start = (f32[56,512]{1,0:T(8,128)S(1)}, f32[56,512]{1,0:T(8,128)S(1)}, u32[]{:S(2)}, u32[]{:S(2)}) collective-permute-start(f32[56,512]{1,0:T(8,128)S(1)} %get-tuple-element.18), channel_id=1, source_target_pairs={{64,0},{128,64},{192,128},{256,192},{320,256},{384,320},{448,384},... | collective-permute-start | bytes 344072 | tf_op jit(solution)/shard_map/ppermute | solution.py:565
  12.5 35.8 %all-to-all-start = ((f32[64,1,1408]{2,1,0:T(1,128)}), f32[64,1,1408]{2,1,0:T(1,128)S(1)}, u32[]{:S(2)}, u32[]{:S(2)}) async-start(f32[64,1,1408]{2,1,0:T(1,128)} %bitcast), calls=%async_computation | async-start | bytes 720896 | tf_op jit(solution)/shard_map/all_to_all | solution.py:570
  30.7 9.6 %collective-permute-start.2 = (f32[40,512]{1,0:T(8,128)S(1)}, f32[40,512]{1,0:T(8,128)S(1)}, u32[]{:S(2)}, u32[]{:S(2)}) collective-permute-start(f32[40,512]{1,0:T(8,128)S(1)} %get-tuple-element.22), channel_id=1, source_target_pairs={{0,1},{1,2},{2,3},{3,4},{4,5},{5,6},{6,7},{7,8},{8,9},{9,10},{10,1... | collective-permute-start | bytes 245768 | tf_op jit(solution)/shard_map/ppermute | solution.py:567
  35.2 8.5 %collective-permute-start.3 = (f32[40,512]{1,0:T(8,128)S(1)}, f32[40,512]{1,0:T(8,128)S(1)}, u32[]{:S(2)}, u32[]{:S(2)}) collective-permute-start(f32[40,512]{1,0:T(8,128)S(1)} %get-tuple-element.23), channel_id=1, source_target_pairs={{1,0},{2,1},{3,2},{4,3},{5,4},{6,5},{7,6},{8,7},{9,8},{10,9},{11,1... | collective-permute-start | bytes 245768 | tf_op jit(solution)/shard_map/ppermute | solution.py:568
  37.1 0.7 %copy-start = (s32[8,512]{1,0:T(8,128)S(1)}, s32[8,512]{1,0:T(8,128)}, u32[]{:S(2)}) copy-start(s32[8,512]{1,0:T(8,128)} %mask.1) | copy-start | bytes 49156
  37.1 0.7 %copy-start.1 = (s32[1,2,1,64]{3,2,1,0:T(1,128)S(1)}, s32[1,2,1,64]{3,2,1,0:T(1,128)}, u32[]{:S(2)}) copy-start(s32[1,2,1,64]{3,2,1,0:T(1,128)} %flags.3) | copy-start | bytes 1540
  37.1 0.7 %copy-start.2 = (s32[1,2]{1,0:T(1,128)S(1)}, s32[1,2]{1,0:T(1,128)}, u32[]{:S(2)}) copy-start(s32[1,2]{1,0:T(1,128)} %codes.1) | copy-start | bytes 28

commit v2 on v1

--- a/solution.py
+++ b/solution.py
@@ -89,7 +89,7 @@
     return moved, after, before
 
 
-def advance_kernel(disp, vel, acc, flags, adv, half, down, up, low, high):
+def advance_kernel(disp, vel, acc, flags, adv, half, one, two, low, high):
     values = []
     for layer in range(4):
         for comp in range(3):
@@ -103,10 +103,11 @@
             values.append(moved)
     low[36:40] = jnp.zeros((4, CELLS), F32)
     high[36:40] = jnp.zeros((4, CELLS), F32)
-    for slot, field in enumerate((1, 0, 2, 4, 3, 5, 8)):
-        down[8 * slot : 8 * slot + 8] = values[field]
-    for slot, field in enumerate((10, 9, 11, 7, 6, 8, 5)):
-        up[8 * slot : 8 * slot + 8] = values[field]
+    even = jnp.bitwise_and(place()[0], 1) == 0
+    for slot, fields in enumerate(zip((1, 0, 2, 4, 3, 5, 8), (10, 9, 11, 7, 6, 8, 5))):
+        to_lower, to_upper = (values[field] for field in fields)
+        one[8 * slot : 8 * slot + 8] = jnp.where(even, to_upper, to_lower)
+        two[8 * slot : 8 * slot + 8] = jnp.where(even, to_lower, to_upper)
     first = flags[0, 0]
     second = flags[0, 1]
     parts = jnp.concatenate(
@@ -116,11 +117,17 @@
     block = lax.broadcasted_iota(I32, (TURNS, CELLS), 0)
     column = lax.broadcasted_iota(I32, (TURNS, CELLS), 1)
     spread = (jnp.right_shift(column, 3) == block).astype(F32)
-    up[56:64] = jnp.dot(parts, spread, precision=lax.Precision.HIGHEST, preferred_element_type=F32)
-
-
-def turn_kernel(above, below, message, turned):
-    stacked = jnp.concatenate([above[...], below[...], jnp.zeros((8, CELLS), F32)], axis=0)
+    spread_parts = jnp.dot(parts, spread, precision=lax.Precision.HIGHEST, preferred_element_type=F32)
+    one[56:64] = spread_parts
+    two[56:64] = spread_parts
+
+
+def turn_kernel(one, two, message, turned):
+    even = jnp.bitwise_and(place()[0], 1) == 0
+    first, second = one[...], two[...]
+    above = jnp.where(even, first[0:56], second[0:56])
+    below = jnp.where(even, second, first)
+    stacked = jnp.concatenate([above, below, jnp.zeros((8, CELLS), F32)], axis=0)
     turned[0:8] = jnp.zeros((8, 128), F32)
     turned[CELLS + 8 : CELLS + 16] = jnp.zeros((8, 128), F32)
     for piece in range(4):
@@ -370,13 +377,14 @@
     def spread(q):
         for slot in (0, 1, 2, 3, 4, 5, 7, 8, 9, 10, 11, 12):
             field = facing[q, 8 * slot : 8 * slot + 8]
-            for dj, other in shifted_by(field, cell)[0].items():
-                moved[dj + 2, slot, q] = other
-
-    def kept(dz, di, dj, spot, value):
+            moved[slot, q, 0:8] = pltpu.roll(field, 1, 1)
+            moved[slot, q, 8:16] = field
+            moved[slot, q, 16:24] = pltpu.roll(field, 127, 1)
+
+    def kept(dz, di, dj, spot):
         k = class_index(dz, -dj, -di)
         whole = jnp.bitwise_and(below[k // 30, dj + 2, spot], 1 << (k % 30)) == 0
-        return jnp.where(whole, weight(dz, di, dj) * value, 0.0)
+        return jnp.where(whole, weight(dz, di, dj), 0.0)
 
     def bonds(m):
         x = [own[field, m] for field in range(12)]
@@ -389,7 +397,7 @@
             pi, pj = turn * di, turn * dj
 
             def y(slot):
-                return moved[dj + 2, slot, q] if dj else facing[q, 8 * slot : 8 * slot + 8]
+                return moved[slot, q, 8 + dj : 16 + dj]
 
             far, far_z = along(pi, pj, y(0), y(1)), y(2)
             near = along(pi, pj, x[9], x[10])
@@ -410,16 +418,17 @@
             far, far_z = along(pi, pj, y(7), y(8)), y(9)
             near = along(pi, pj, x[0], x[1])
             value, sign = stretched(turn, far, near, -1, far_z, x[2])
-            first = kept(1, di, dj, q, value)
+            first = kept(1, di, dj, q) * value
             grown(sums, 2, -sign, first)
             plane = first
             if close:
                 value, sign = stretched(turn, along(pi, pj, y(10), y(11)), near, -2, y(12), x[2])
-                second = kept(2, di, dj, q, value)
+                strength = kept(2, di, dj, q)
+                second = strength * value
                 grown(double, 2, -sign, second)
                 plane = first + second
                 value, sign = stretched(turn, far, along(pi, pj, x[3], x[4]), -2, far_z, x[5])
-                second = kept(2, di, dj, q, value)
+                second = strength * value
                 grown(double, 5, -sign, second)
                 pushed(sums, wide, 3, di, dj, sign, second)
             pushed(sums, wide, 0, di, dj, sign, plane)
@@ -428,9 +437,10 @@
                 grown(sums, 11, 1, rise * (facing[q, 48:56] - x[11]))
                 grown(sums, 8, 1, rise * (y(5) - x[8]))
                 grown(sums, 5, 1, rise * (y(2) - x[5]))
-                grown(sums, 2, 1, kept(3, 0, 0, q, 9.0 * (facing[q, 104:112] - x[2])))
-                grown(sums, 5, 1, kept(3, 0, 0, q, 9.0 * (y(12) - x[5])))
-                grown(sums, 8, 1, kept(3, 0, 0, q, 9.0 * (y(9) - x[8])))
+                rise = 9.0 * kept(3, 0, 0, q)
+                grown(sums, 2, 1, rise * (facing[q, 104:112] - x[2]))
+                grown(sums, 5, 1, rise * (y(12) - x[5]))
+                grown(sums, 8, 1, rise * (y(9) - x[8]))
         for extra in (wide, double):
             for field, value in extra.items():
                 sums[field] = sums[field] + 2.0 * value
@@ -479,7 +489,7 @@
         out_shape=(
             near(3, 1, 4, ROWS, CELLS),
             near(3, 1, 4, ROWS, CELLS),
-            near(56, CELLS),
+            near(64, CELLS),
             near(64, CELLS),
             near(40, CELLS),
             near(40, CELLS),
@@ -488,14 +498,14 @@
     )(displacement, velocity, acceleration, flags)
 
 
-def run_turn(above, below):
+def run_turn(one, two):
     return pl.pallas_call(
         turn_kernel,
         out_shape=near(TURNS * WINDOW, 128),
         scratch_shapes=[pltpu.VMEM((CELLS + 16, 128), F32)],
         interpret=INTERPRET,
         compiler_params=pltpu.CompilerParams(vmem_limit_bytes=16 * 1024 * 1024),
-    )(kept_near(above), kept_near(below))
+    )(kept_near(one), kept_near(two))
 
 
 def run_pair(adv, codes, flags, mask):
@@ -545,7 +555,7 @@
         out_shape=(shape(3, 1, 4, ROWS, CELLS), shape(3, 1, 4, ROWS, CELLS)),
         scratch_shapes=[
             pltpu.VMEM((8, 128, 128), F32),
-            pltpu.VMEM((5, 13, 8, 8, 128), F32),
+            pltpu.VMEM((13, 8, 24, 128), F32),
             pltpu.VMEM((2, 5, 8, 8, 128), I32),
             pltpu.VMEM((96, 8, 128), F32),
             pltpu.VMEM((CELLS, 128), F32),
@@ -560,13 +570,19 @@
     return [(i, i + by) for i in range(count) if 0 <= i + by < count]
 
 
+def swaps(axis, start):
+    count = lax.axis_size(axis)
+    pairs = [(i, i + 1) for i in range(start, count - 1, 2)]
+    return pairs + [(j, i) for i, j in pairs]
+
+
 def local(displacement, velocity, acceleration, fibre_codes, contact_mask, bond_flags):
-    adv, half, down, up, low, high = run_advance(displacement, velocity, acceleration, bond_flags)
-    above = lax.ppermute(down, "ply", steps("ply", -1))
-    below = lax.ppermute(up, "ply", steps("ply", 1))
+    adv, half, one, two, low, high = run_advance(displacement, velocity, acceleration, bond_flags)
+    one = lax.ppermute(one, "ply", swaps("ply", 0))
+    two = lax.ppermute(two, "ply", swaps("ply", 1))
     low = lax.ppermute(low, "stripe", steps("stripe", 1))
     high = lax.ppermute(high, "stripe", steps("stripe", -1))
-    message = run_turn(above, below).reshape(TURNS, 1, WINDOW * 128)
+    message = run_turn(one, two).reshape(TURNS, 1, WINDOW * 128)
     message = lax.all_to_all(message, "stripe", 0, 0)
     partial, own, strengths, rates, present, impact = run_pair(adv, fibre_codes, bond_flags, contact_mask)
     force = run_edge(low, high, own, rates, present, partial)

time: 50.9 us -> 50.2 us (0.986)
  the two profiles are of different devices: /device:TPU:1 before, /device:TPU:7 now
where the time goes in v2:
time: 50.2 us; the launch traced here: 49.9 us
  starting transfers between devices  30.8 us (61%)
  waiting for transfers between devices  9.69 us (19%)
  Pallas kernels  7.92 us (16%)
  between operations  0.72 us (1%)
  local copies, waits for them, and re-layouts  0.7 us (1%)
    all_to_all x1, starting transfers between devices, local(): message = lax.all_to_all(message, 'stripe', 0, 0)  18.2 us
    ppermute x1, starting transfers between devices, local(): low = lax.ppermute(low, 'stripe', steps('stripe', 1))  4.44 us
    ppermute x1, waiting for transfers between devices, local(): two = lax.ppermute(two, 'ply', swaps('ply', 1))  4.01 us
    all_to_all x1, waiting for transfers between devices, local(): message = lax.all_to_all(message, 'stripe', 0, 0)  3.87 us
    ppermute x1, starting transfers between devices, local(): two = lax.ppermute(two, 'ply', swaps('ply', 1))  3.78 us
    pallas_call x1, Pallas kernels, run_pair(): pl.pallas_call(pair_kernel, out_shape=(near(12, 4, 8, 128), near(12, 8, 8...  2.5 us
    ppermute x1, starting transfers between devices, local(): one = lax.ppermute(one, 'ply', swaps('ply', 0))  2.46 us
    pallas_call x1, Pallas kernels, run_interface(): pl.pallas_call(interface_kernel, out_shape=(shape(3, 1, 4, ROWS, CELLS),...  2.04 us
  transfers between devices with their start and end apart: 5, of which 3 were waited for; matrix products, arithmetic and copies ran while one was open for 1% of the time, Pallas kernels for 7%

profile of v2, /device:TPU:7, one launch (start us, length us, event | category | flops | bytes accessed | tf_op | source)
XLA Modules:
  0.0 49.9 jit_solution(8211896898344286037)
XLA Ops:
  0.6 1.4 %shard_map.85 = (f32[3,1,4,8,512]{4,3,2,1,0:T(8,128)S(1)}, f32[3,1,4,8,512]{4,3,2,1,0:T(8,128)S(1)}, f32[64,512]{1,0:T(8,128)S(1)}, f32[64,512]{1,0:T(8,128)S(1)...) custom-call(f32[3,1,4,8,512]{4,3,2,1,0:T(8,128)} %disp.1, f32[3,1,4,8,512]{4,3,2,1,0:T(8,128)} %vel.1, ...), custom_call_target="tpu_custom_call" | custom-call | tf_op jit(solution)/shard_map/pallas_call | solution.py:487
  2.0 2.5 %collective-permute-start = (f32[64,512]{1,0:T(8,128)S(1)}, f32[64,512]{1,0:T(8,128)S(1)}, u32[]{:S(2)}, u32[]{:S(2)}) collective-permute-start(f32[64,512]{1,0:T(8,128)S(1)} %get-tuple-element.18), channel_id=1, source_target_pairs={{0,64},{128,192},{256,320},{384,448},{64,0},{192,128},{320,256},{4... | collective-permute-start | bytes 393224 | tf_op jit(solution)/shard_map/ppermute | solution.py:581
  4.5 3.8 %collective-permute-start.1 = (f32[64,512]{1,0:T(8,128)S(1)}, f32[64,512]{1,0:T(8,128)S(1)}, u32[]{:S(2)}, u32[]{:S(2)}) collective-permute-start(f32[64,512]{1,0:T(8,128)S(1)} %get-tuple-element.19), channel_id=1, source_target_pairs={{64,128},{192,256},{320,384},{128,64},{256,192},{384,320},{65,129}... | collective-permute-start | bytes 393224 | tf_op jit(solution)/shard_map/ppermute | solution.py:582
  8.2 0.0 collective-permute-done.one
  8.3 4.0 %collective-permute-done.1.two = f32[64,512]{1,0:T(8,128)S(1)} collective-permute-done((f32[64,512]{1,0:T(8,128)S(1)}, f32[64,512]{1,0:T(8,128)S(1)}, u32[]{:S(2)}, u32[]{:S(2)}) %collective-permute-start.1) | collective-permute-done | bytes 131104 | tf_op jit(solution)/shard_map/ppermute | solution.py:582
  12.3 1.0 %shard_map.86 = f32[704,128]{1,0:T(8,128)} custom-call(f32[64,512]{1,0:T(8,128)S(1)} %collective-permute-done.one, f32[64,512]{1,0:T(8,128)S(1)} %collective-permute-done.1.two), custom_call_target="tpu_custom_call" | custom-call | tf_op jit(solution)/shard_map/pallas_call | solution.py:502
  13.3 18.2 %all-to-all-start = ((f32[64,1,1408]{2,1,0:T(1,128)}), f32[64,1,1408]{2,1,0:T(1,128)S(1)}, u32[]{:S(2)}, u32[]{:S(2)}) async-start(f32[64,1,1408]{2,1,0:T(1,128)} %bitcast), calls=%async_computation | async-start | bytes 720896 | tf_op jit(solution)/shard_map/all_to_all | solution.py:586
  31.5 4.4 %collective-permute-start.2 = (f32[40,512]{1,0:T(8,128)S(1)}, f32[40,512]{1,0:T(8,128)S(1)}, u32[]{:S(2)}, u32[]{:S(2)}) collective-permute-start(f32[40,512]{1,0:T(8,128)S(1)} %get-tuple-element.22), channel_id=1, source_target_pairs={{0,1},{1,2},{2,3},{3,4},{4,5},{5,6},{6,7},{7,8},{8,9},{9,10},{10,1... | collective-permute-start | bytes 245768 | tf_op jit(solution)/shard_map/ppermute | solution.py:583
  36.0 1.9 %collective-permute-start.3 = (f32[40,512]{1,0:T(8,128)S(1)}, f32[40,512]{1,0:T(8,128)S(1)}, u32[]{:S(2)}, u32[]{:S(2)}) collective-permute-start(f32[40,512]{1,0:T(8,128)S(1)} %get-tuple-element.23), channel_id=1, source_target_pairs={{1,0},{2,1},{3,2},{4,3},{5,4},{6,5},{7,6},{8,7},{9,8},{10,9},{11,1... | collective-permute-start | bytes 245768 | tf_op jit(solution)/shard_map/ppermute | solution.py:584
  37.9 0.0 copy-start
  37.9 0.0 copy-start.1
  37.9 0.0 copy-start.2
  37.9 0.7 %copy.10 = f32[3,1,4,8,512]{4,3,2,1,0:T(8,128)} copy(f32[3,1,4,8,512]{4,3,2,1,0:T(8,128)S(1)} %get-tuple-element.31.adv) | data formatting | bytes 393216
  38.6 0.0 copy-done
  38.6 0.0 copy-done.1
  38.6 0.0 copy-done.2
  38.6 2.5 %shard_map.87 = (f32[12,4,8,128]{3,2,1,0:T(8,128)S(1)}, f32[12,8,8,128]{3,2,1,0:T(8,128)S(1)}, f32[2,26,4,8,128]{4,3,2,1,0:T(8,128)S(1)}, f32[26,6,8,128]{3,2,1,...) custom-call(f32[3,1,4,8,512]{4,3,2,1,0:T(8,128)S(1)} %get-tuple-element.31.adv, ...), custom_call_target="tpu_custom_call" | custom-call | flops 20000000 | bytes 1000000 | tf_op jit(solution)/shard_map/pallas_call | solution.py:513
  41.1 0.0 collective-permute-done.2.low
  41.1 1.8 %collective-permute-done.3.high = f32[40,512]{1,0:T(8,128)S(1)} collective-permute-done((f32[40,512]{1,0:T(8,128)S(1)}, f32[40,512]{1,0:T(8,128)S(1)}, u32[]{:S(2)}, u32[]{:S(2)}) %collective-permute-start.3) | collective-permute-done | bytes 81952 | tf_op jit(solution)/shard_map/ppermute | solution.py:584
  42.9 1.0 %shard_map.88.force = f32[12,4,8,128]{3,2,1,0:T(8,128)S(1)} custom-call(f32[40,512]{1,0:T(8,128)S(1)} %collective-permute-done.2.low, f32[40,512]{1,0:T(8,128)S(1)} %collective-permute-done.3.high, f32[12,8,8,128]{3,2,1,0:T(8,128)S(1)} %get-tuple-element.20.base.own, f32[26,6,8,128]{3,2,1,0:T(8,128)S(1)} %get-tuple-element.24.rates, ...), custom_call_target="tpu_custom_call" | custom-call | flops 10000000 | bytes 1000000 | tf_op jit(solution)/shard_map/pallas_call | solution.py:538
  43.9 3.9 %all-to-all-done = f32[64,1,1408]{2,1,0:T(1,128)S(1)} async-done(((f32[64,1,1408]{2,1,0:T(1,128)}), f32[64,1,1408]{2,1,0:T(1,128)S(1)}, u32[]{:S(2)}, u32[]{:S(2)}) %all-to-all-start) | async-done | bytes 360480 | tf_op jit(solution)/shard_map/all_to_all | solution.py:586
  47.8 2.0 %shard_map.89 = (f32[3,1,4,8,512]{4,3,2,1,0:T(8,128)}, f32[3,1,4,8,512]{4,3,2,1,0:T(8,128)}) custom-call(f32[704,128]{1,0:T(8,128)S(1)} %bitcast.2, f32[12,8,8,128]{3,2,1,0:T(8,128)S(1)} %get-tuple-element.20.base.own, f32[2,26,4,8,128]{4,3,2,1,0:T(8,128)S(1)} %get-tuple-element.21.strengths, f32[12,4,8,128]{3,2,1,0:T(8,128)S(1)} %shard_map.88.force, ...), custom_call_target="tpu_custom_call" | custom-call | tf_op jit(solution)/shard_map/pallas_call | solution.py:553
Async XLA Ops:
  2.0 6.3 %collective-permute-start = (f32[64,512]{1,0:T(8,128)S(1)}, f32[64,512]{1,0:T(8,128)S(1)}, u32[]{:S(2)}, u32[]{:S(2)}) collective-permute-start(f32[64,512]{1,0:T(8,128)S(1)} %get-tuple-element.18), channel_id=1, source_target_pairs={{0,64},{128,192},{256,320},{384,448},{64,0},{192,128},{320,256},{4... | collective-permute-start | bytes 393224 | tf_op jit(solution)/shard_map/ppermute | solution.py:581
  4.5 7.8 %collective-permute-start.1 = (f32[64,512]{1,0:T(8,128)S(1)}, f32[64,512]{1,0:T(8,128)S(1)}, u32[]{:S(2)}, u32[]{:S(2)}) collective-permute-start(f32[64,512]{1,0:T(8,128)S(1)} %get-tuple-element.19), channel_id=1, source_target_pairs={{64,128},{192,256},{320,384},{128,64},{256,192},{384,320},{65,129}... | collective-permute-start | bytes 393224 | tf_op jit(solution)/shard_map/ppermute | solution.py:582
  13.3 34.5 %all-to-all-start = ((f32[64,1,1408]{2,1,0:T(1,128)}), f32[64,1,1408]{2,1,0:T(1,128)S(1)}, u32[]{:S(2)}, u32[]{:S(2)}) async-start(f32[64,1,1408]{2,1,0:T(1,128)} %bitcast), calls=%async_computation | async-start | bytes 720896 | tf_op jit(solution)/shard_map/all_to_all | solution.py:586
  31.5 9.6 %collective-permute-start.2 = (f32[40,512]{1,0:T(8,128)S(1)}, f32[40,512]{1,0:T(8,128)S(1)}, u32[]{:S(2)}, u32[]{:S(2)}) collective-permute-start(f32[40,512]{1,0:T(8,128)S(1)} %get-tuple-element.22), channel_id=1, source_target_pairs={{0,1},{1,2},{2,3},{3,4},{4,5},{5,6},{6,7},{7,8},{8,9},{9,10},{10,1... | collective-permute-start | bytes 245768 | tf_op jit(solution)/shard_map/ppermute | solution.py:583
  36.0 7.0 %collective-permute-start.3 = (f32[40,512]{1,0:T(8,128)S(1)}, f32[40,512]{1,0:T(8,128)S(1)}, u32[]{:S(2)}, u32[]{:S(2)}) collective-permute-start(f32[40,512]{1,0:T(8,128)S(1)} %get-tuple-element.23), channel_id=1, source_target_pairs={{1,0},{2,1},{3,2},{4,3},{5,4},{6,5},{7,6},{8,7},{9,8},{10,9},{11,1... | collective-permute-start | bytes 245768 | tf_op jit(solution)/shard_map/ppermute | solution.py:584
  37.9 0.7 %copy-start = (s32[8,512]{1,0:T(8,128)S(1)}, s32[8,512]{1,0:T(8,128)}, u32[]{:S(2)}) copy-start(s32[8,512]{1,0:T(8,128)} %mask.1) | copy-start | bytes 49156
  37.9 0.7 %copy-start.1 = (s32[1,2,1,64]{3,2,1,0:T(1,128)S(1)}, s32[1,2,1,64]{3,2,1,0:T(1,128)}, u32[]{:S(2)}) copy-start(s32[1,2,1,64]{3,2,1,0:T(1,128)} %flags.3) | copy-start | bytes 1540
  37.9 0.7 %copy-start.2 = (s32[1,2]{1,0:T(1,128)S(1)}, s32[1,2]{1,0:T(1,128)}, u32[]{:S(2)}) copy-start(s32[1,2]{1,0:T(1,128)} %codes.1) | copy-start | bytes 28

commit v3 on v2

--- a/solution.py
+++ b/solution.py
@@ -97,12 +97,13 @@
             moved = disp[comp, 0, layer] + speed
             half[comp, 0, layer] = speed
             adv[comp, 0, layer] = moved
-            field = 3 * layer + comp
-            low[3 * field : 3 * field + 3] = moved[5:8]
-            high[3 * field : 3 * field + 3] = moved[0:3]
+            count = 2 if comp else 3
+            start = 7 * layer + (0, 3, 5)[comp]
+            low[start : start + count] = moved[8 - count : 8]
+            high[start : start + count] = moved[0:count]
             values.append(moved)
-    low[36:40] = jnp.zeros((4, CELLS), F32)
-    high[36:40] = jnp.zeros((4, CELLS), F32)
+    low[28:32] = jnp.zeros((4, CELLS), F32)
+    high[28:32] = jnp.zeros((4, CELLS), F32)
     even = jnp.bitwise_and(place()[0], 1) == 0
     for slot, fields in enumerate(zip((1, 0, 2, 4, 3, 5, 8), (10, 9, 11, 7, 6, 8, 5))):
         to_lower, to_upper = (values[field] for field in fields)
@@ -279,14 +280,17 @@
     left = lane < TURNS
     for side, rows in enumerate((low, high)):
         for piece in range(4):
-            turned[side, 128 * piece : 128 * piece + 128, 0:40] = rows[:, 128 * piece : 128 * piece + 128].T
+            turned[side, 128 * piece : 128 * piece + 128, 0:32] = rows[:, 128 * piece : 128 * piece + 128].T
     for position in range(8):
         pick = pl.ds(position, TURNS, stride=8)
         both = jnp.concatenate([turned[0, pick, :], turned[1, pick, :]], axis=0)
-        held[40 * position : 40 * position + 40] = both.T[0:40]
+        held[32 * position : 32 * position + 32] = both.T[0:32]
 
     def around(field, q):
-        other = held[pl.ds(3 * field + (q + 3 if q < 0 else q - 4), 8, stride=40), :]
+        layer, comp = field // 3, field % 3
+        count = 2 if comp else 3
+        start = 7 * layer + (0, 3, 5)[comp]
+        other = held[pl.ds(start + (q + count if q < 0 else q - 4), 8, stride=32), :]
         return jnp.where(left, other, base[field, q + 8]) if q < 0 else jnp.where(left, base[field, q], other)
 
     for field in range(12):
@@ -491,8 +495,8 @@
             near(3, 1, 4, ROWS, CELLS),
             near(64, CELLS),
             near(64, CELLS),
-            near(40, CELLS),
-            near(40, CELLS),
+            near(32, CELLS),
+            near(32, CELLS),
         ),
         interpret=INTERPRET,
     )(displacement, velocity, acceleration, flags)
@@ -540,7 +544,7 @@
         out_shape=near(12, 4, 8, 128),
         scratch_shapes=[
             pltpu.VMEM((2, CELLS, 128), F32),
-            pltpu.VMEM((8 * 40, 128), F32),
+            pltpu.VMEM((8 * 32, 128), F32),
             pltpu.VMEM((5, 12, 4, 8, 128), F32),
         ],
         interpret=INTERPRET,

time: 50.2 us -> 50.2 us (level)
  no operation moved by 1% of the time
where the time goes in v3:
time: 50.2 us; the launch traced here: 49.8 us
  starting transfers between devices  30.8 us (61%)
  waiting for transfers between devices  9.54 us (19%)
  Pallas kernels  7.97 us (16%)
  between operations  0.72 us (1%)
  local copies, waits for them, and re-layouts  0.7 us (1%)
    all_to_all x1, starting transfers between devices, local(): message = lax.all_to_all(message, 'stripe', 0, 0)  18.2 us
    ppermute x1, starting transfers between devices, local(): low = lax.ppermute(low, 'stripe', steps('stripe', 1))  4.44 us
    ppermute x1, waiting for transfers between devices, local(): two = lax.ppermute(two, 'ply', swaps('ply', 1))  4.01 us
    all_to_all x1, waiting for transfers between devices, local(): message = lax.all_to_all(message, 'stripe', 0, 0)  3.9 us
    ppermute x1, starting transfers between devices, local(): two = lax.ppermute(two, 'ply', swaps('ply', 1))  3.78 us
    pallas_call x1, Pallas kernels, run_pair(): pl.pallas_call(pair_kernel, out_shape=(near(12, 4, 8, 128), near(12, 8, 8...  2.5 us
    ppermute x1, starting transfers between devices, local(): one = lax.ppermute(one, 'ply', swaps('ply', 0))  2.46 us
    pallas_call x1, Pallas kernels, run_interface(): pl.pallas_call(interface_kernel, out_shape=(shape(3, 1, 4, ROWS, CELLS),...  2.04 us
  transfers between devices with their start and end apart: 5, of which 3 were waited for; matrix products, arithmetic and copies ran while one was open for 1% of the time, Pallas kernels for 7%

profile of v3, /device:TPU:7, one launch (start us, length us, event | category | flops | bytes accessed | tf_op | source)
XLA Modules:
  0.0 49.8 jit_solution(1233670688589549443)
XLA Ops:
  0.6 1.4 %shard_map.85 = (f32[3,1,4,8,512]{4,3,2,1,0:T(8,128)S(1)}, f32[3,1,4,8,512]{4,3,2,1,0:T(8,128)S(1)}, f32[64,512]{1,0:T(8,128)S(1)}, f32[64,512]{1,0:T(8,128)S(1)...) custom-call(f32[3,1,4,8,512]{4,3,2,1,0:T(8,128)} %disp.1, f32[3,1,4,8,512]{4,3,2,1,0:T(8,128)} %vel.1, ...), custom_call_target="tpu_custom_call" | custom-call | tf_op jit(solution)/shard_map/pallas_call | solution.py:491
  2.0 2.5 %collective-permute-start = (f32[64,512]{1,0:T(8,128)S(1)}, f32[64,512]{1,0:T(8,128)S(1)}, u32[]{:S(2)}, u32[]{:S(2)}) collective-permute-start(f32[64,512]{1,0:T(8,128)S(1)} %get-tuple-element.18), channel_id=1, source_target_pairs={{0,64},{128,192},{256,320},{384,448},{64,0},{192,128},{320,256},{4... | collective-permute-start | bytes 393224 | tf_op jit(solution)/shard_map/ppermute | solution.py:585
  4.5 3.8 %collective-permute-start.1 = (f32[64,512]{1,0:T(8,128)S(1)}, f32[64,512]{1,0:T(8,128)S(1)}, u32[]{:S(2)}, u32[]{:S(2)}) collective-permute-start(f32[64,512]{1,0:T(8,128)S(1)} %get-tuple-element.19), channel_id=1, source_target_pairs={{64,128},{192,256},{320,384},{128,64},{256,192},{384,320},{65,129}... | collective-permute-start | bytes 393224 | tf_op jit(solution)/shard_map/ppermute | solution.py:586
  8.2 0.0 collective-permute-done.one
  8.3 4.0 %collective-permute-done.1.two = f32[64,512]{1,0:T(8,128)S(1)} collective-permute-done((f32[64,512]{1,0:T(8,128)S(1)}, f32[64,512]{1,0:T(8,128)S(1)}, u32[]{:S(2)}, u32[]{:S(2)}) %collective-permute-start.1) | collective-permute-done | bytes 131104 | tf_op jit(solution)/shard_map/ppermute | solution.py:586
  12.3 1.0 %shard_map.86 = f32[704,128]{1,0:T(8,128)} custom-call(f32[64,512]{1,0:T(8,128)S(1)} %collective-permute-done.one, f32[64,512]{1,0:T(8,128)S(1)} %collective-permute-done.1.two), custom_call_target="tpu_custom_call" | custom-call | tf_op jit(solution)/shard_map/pallas_call | solution.py:506
  13.3 18.2 %all-to-all-start = ((f32[64,1,1408]{2,1,0:T(1,128)}), f32[64,1,1408]{2,1,0:T(1,128)S(1)}, u32[]{:S(2)}, u32[]{:S(2)}) async-start(f32[64,1,1408]{2,1,0:T(1,128)} %bitcast), calls=%async_computation | async-start | bytes 720896 | tf_op jit(solution)/shard_map/all_to_all | solution.py:590
  31.5 4.4 %collective-permute-start.2 = (f32[32,512]{1,0:T(8,128)S(1)}, f32[32,512]{1,0:T(8,128)S(1)}, u32[]{:S(2)}, u32[]{:S(2)}) collective-permute-start(f32[32,512]{1,0:T(8,128)S(1)} %get-tuple-element.22), channel_id=1, source_target_pairs={{0,1},{1,2},{2,3},{3,4},{4,5},{5,6},{6,7},{7,8},{8,9},{9,10},{10,1... | collective-permute-start | bytes 196616 | tf_op jit(solution)/shard_map/ppermute | solution.py:587
  36.0 1.9 %collective-permute-start.3 = (f32[32,512]{1,0:T(8,128)S(1)}, f32[32,512]{1,0:T(8,128)S(1)}, u32[]{:S(2)}, u32[]{:S(2)}) collective-permute-start(f32[32,512]{1,0:T(8,128)S(1)} %get-tuple-element.23), channel_id=1, source_target_pairs={{1,0},{2,1},{3,2},{4,3},{5,4},{6,5},{7,6},{8,7},{9,8},{10,9},{11,1... | collective-permute-start | bytes 196616 | tf_op jit(solution)/shard_map/ppermute | solution.py:588
  37.9 0.0 copy-start
  37.9 0.0 copy-start.1
  37.9 0.0 copy-start.2
  37.9 0.7 %copy.10 = f32[3,1,4,8,512]{4,3,2,1,0:T(8,128)} copy(f32[3,1,4,8,512]{4,3,2,1,0:T(8,128)S(1)} %get-tuple-element.31.adv) | data formatting | bytes 393216
  38.6 0.0 copy-done
  38.6 0.0 copy-done.1
  38.6 0.0 copy-done.2
  38.6 2.5 %shard_map.87 = (f32[12,4,8,128]{3,2,1,0:T(8,128)S(1)}, f32[12,8,8,128]{3,2,1,0:T(8,128)S(1)}, f32[2,26,4,8,128]{4,3,2,1,0:T(8,128)S(1)}, f32[26,6,8,128]{3,2,1,...) custom-call(f32[3,1,4,8,512]{4,3,2,1,0:T(8,128)S(1)} %get-tuple-element.31.adv, ...), custom_call_target="tpu_custom_call" | custom-call | flops 20000000 | bytes 1000000 | tf_op jit(solution)/shard_map/pallas_call | solution.py:517
  41.1 0.0 collective-permute-done.2.low
  41.1 1.6 %collective-permute-done.3.high = f32[32,512]{1,0:T(8,128)S(1)} collective-permute-done((f32[32,512]{1,0:T(8,128)S(1)}, f32[32,512]{1,0:T(8,128)S(1)}, u32[]{:S(2)}, u32[]{:S(2)}) %collective-permute-start.3) | collective-permute-done | bytes 65568 | tf_op jit(solution)/shard_map/ppermute | solution.py:588
  42.8 1.1 %shard_map.88.force = f32[12,4,8,128]{3,2,1,0:T(8,128)S(1)} custom-call(f32[32,512]{1,0:T(8,128)S(1)} %collective-permute-done.2.low, f32[32,512]{1,0:T(8,128)S(1)} %collective-permute-done.3.high, f32[12,8,8,128]{3,2,1,0:T(8,128)S(1)} %get-tuple-element.20.base.own, f32[26,6,8,128]{3,2,1,0:T(8,128)S(1)} %get-tuple-element.24.rates, ...), custom_call_target="tpu_custom_call" | custom-call | flops 10000000 | bytes 1000000 | tf_op jit(solution)/shard_map/pallas_call | solution.py:542
  43.8 3.9 %all-to-all-done = f32[64,1,1408]{2,1,0:T(1,128)S(1)} async-done(((f32[64,1,1408]{2,1,0:T(1,128)}), f32[64,1,1408]{2,1,0:T(1,128)S(1)}, u32[]{:S(2)}, u32[]{:S(2)}) %all-to-all-start) | async-done | bytes 360480 | tf_op jit(solution)/shard_map/all_to_all | solution.py:590
  47.7 2.0 %shard_map.89 = (f32[3,1,4,8,512]{4,3,2,1,0:T(8,128)}, f32[3,1,4,8,512]{4,3,2,1,0:T(8,128)}) custom-call(f32[704,128]{1,0:T(8,128)S(1)} %bitcast.2, f32[12,8,8,128]{3,2,1,0:T(8,128)S(1)} %get-tuple-element.20.base.own, f32[2,26,4,8,128]{4,3,2,1,0:T(8,128)S(1)} %get-tuple-element.21.strengths, f32[12,4,8,128]{3,2,1,0:T(8,128)S(1)} %shard_map.88.force, ...), custom_call_target="tpu_custom_call" | custom-call | tf_op jit(solution)/shard_map/pallas_call | solution.py:557
Async XLA Ops:
  2.0 6.3 %collective-permute-start = (f32[64,512]{1,0:T(8,128)S(1)}, f32[64,512]{1,0:T(8,128)S(1)}, u32[]{:S(2)}, u32[]{:S(2)}) collective-permute-start(f32[64,512]{1,0:T(8,128)S(1)} %get-tuple-element.18), channel_id=1, source_target_pairs={{0,64},{128,192},{256,320},{384,448},{64,0},{192,128},{320,256},{4... | collective-permute-start | bytes 393224 | tf_op jit(solution)/shard_map/ppermute | solution.py:585
  4.5 7.8 %collective-permute-start.1 = (f32[64,512]{1,0:T(8,128)S(1)}, f32[64,512]{1,0:T(8,128)S(1)}, u32[]{:S(2)}, u32[]{:S(2)}) collective-permute-start(f32[64,512]{1,0:T(8,128)S(1)} %get-tuple-element.19), channel_id=1, source_target_pairs={{64,128},{192,256},{320,384},{128,64},{256,192},{384,320},{65,129}... | collective-permute-start | bytes 393224 | tf_op jit(solution)/shard_map/ppermute | solution.py:586
  13.3 34.4 %all-to-all-start = ((f32[64,1,1408]{2,1,0:T(1,128)}), f32[64,1,1408]{2,1,0:T(1,128)S(1)}, u32[]{:S(2)}, u32[]{:S(2)}) async-start(f32[64,1,1408]{2,1,0:T(1,128)} %bitcast), calls=%async_computation | async-start | bytes 720896 | tf_op jit(solution)/shard_map/all_to_all | solution.py:590
  31.5 9.6 %collective-permute-start.2 = (f32[32,512]{1,0:T(8,128)S(1)}, f32[32,512]{1,0:T(8,128)S(1)}, u32[]{:S(2)}, u32[]{:S(2)}) collective-permute-start(f32[32,512]{1,0:T(8,128)S(1)} %get-tuple-element.22), channel_id=1, source_target_pairs={{0,1},{1,2},{2,3},{3,4},{4,5},{5,6},{6,7},{7,8},{8,9},{9,10},{10,1... | collective-permute-start | bytes 196616 | tf_op jit(solution)/shard_map/ppermute | solution.py:587
  36.0 6.8 %collective-permute-start.3 = (f32[32,512]{1,0:T(8,128)S(1)}, f32[32,512]{1,0:T(8,128)S(1)}, u32[]{:S(2)}, u32[]{:S(2)}) collective-permute-start(f32[32,512]{1,0:T(8,128)S(1)} %get-tuple-element.23), channel_id=1, source_target_pairs={{1,0},{2,1},{3,2},{4,3},{5,4},{6,5},{7,6},{8,7},{9,8},{10,9},{11,1... | collective-permute-start | bytes 196616 | tf_op jit(solution)/shard_map/ppermute | solution.py:588
  37.9 0.7 %copy-start = (s32[8,512]{1,0:T(8,128)S(1)}, s32[8,512]{1,0:T(8,128)}, u32[]{:S(2)}) copy-start(s32[8,512]{1,0:T(8,128)} %mask.1) | copy-start | bytes 49156
  37.9 0.7 %copy-start.1 = (s32[1,2,1,64]{3,2,1,0:T(1,128)S(1)}, s32[1,2,1,64]{3,2,1,0:T(1,128)}, u32[]{:S(2)}) copy-start(s32[1,2,1,64]{3,2,1,0:T(1,128)} %flags.3) | copy-start | bytes 1540
  37.9 0.7 %copy-start.2 = (s32[1,2]{1,0:T(1,128)S(1)}, s32[1,2]{1,0:T(1,128)}, u32[]{:S(2)}) copy-start(s32[1,2]{1,0:T(1,128)} %codes.1) | copy-start | bytes 28
